TPU v7x, 512 devices: a whole 4x4x16 slice. The times are simulated.
512 devices in a mesh: tm: 32 (over z, core), rows: 8 (over x, y_lo), cols: 2 (over y_hi).
Axes of the slice: x: 4, y: 4 (y_hi: 2, y_lo: 2; y = y_hi * 2 + y_lo), z: 16, core: 2. Of those that a mesh axis runs over, the one named last changes fastest.
Arguments:
- iterate: float32 [1024, 8, 4, 128], P('tm', 'rows', 'cols'), may hold values from -6 to 6
- source: float32 [1024, 8, 4, 128], P('tm', 'rows', 'cols'), may hold values from -120 to 120
- initial: float32 [8, 4, 128], P('rows', 'cols'), may hold values from -6 to 6
- tile_basis: float32 [8, 4, 128, 128], P('rows', 'cols'), may hold values from -1 to 1, as said below
- tile_values: float32 [8, 4, 128], P('rows', 'cols'), may hold values from 16 to 48
- capacity: float32 [8, 4], P('rows', 'cols'), may hold values from 1 to 20
- tile_links: int32 [4, 8, 4, 128], P(None, 'rows', 'cols'), may hold values from 0 to 127
- conductance: float32 [4, 8, 4, 128], P(None, 'rows', 'cols'), may hold values from 0.5 to 3
Outputs:
- updated: float32 [1024, 8, 4, 128], P('tm', 'rows', 'cols')
Inputs may be any that keep to these rules, and one draw needn't show every extreme that they name: `tile_basis`: each tile's basis has orthonormal columns.
All inputs are finite; a program needn't handle non-finite values.
Results may differ from a plain program's by a relative error of at most 0.0003.
Values sent between devices are 32-bit elements; how exact they have to be, the bound alone decides.
No kernel may reach another device: no remote copies, remote signals or barrier semaphores. Data moves between devices by JAX's collectives and lax.ppermute only.
A program may use at most 64 MiB of HBM per device.

v0:
```python
import math

import jax
import jax.numpy as jnp
from jax import lax
from jax.sharding import PartitionSpec as P

circulant_alpha = 0.05
highest = lax.Precision.HIGHEST


def extended(array, sides, width):
    edges = {}
    for axis, dim in sides:
        count, length = (lax.axis_size(axis), array.shape[dim])
        up = [(i, (i + 1) % count) for i in range(count - 1)]
        last = lax.slice_in_dim(array, length - width, length, axis=dim)
        first = lax.slice_in_dim(array, 0, width, axis=dim)
        edges[dim] = (
            lax.ppermute(last, axis, up),
            lax.ppermute(first, axis, [(b, a) for a, b in up]),
        )
    done = []
    for _, dim in sides:
        low, high = edges[dim]
        around = [(width, width) if d in done else (0, 0) for d in range(array.ndim)]
        array = jnp.concatenate([jnp.pad(low, around), array, jnp.pad(high, around)], axis=dim)
        done.append(dim)
    return array


def from_behind(array, axis, by):
    count = lax.axis_size(axis)
    pairs = [(i, i + by) for i in range(count) if 0 <= i + by < count]
    return lax.ppermute(array, axis, pairs)


def couple(field, tile_links, conductance):
    tile_rows = field.shape[1]
    tile_cols = field.shape[2]
    padded = extended(field, (("rows", 1), ("cols", 2)), 1)
    beside = (
        padded[:, 0:tile_rows, 1 : tile_cols + 1],
        padded[:, 2 : tile_rows + 2, 1 : tile_cols + 1],
        padded[:, 1 : tile_rows + 1, 0:tile_cols],
        padded[:, 1 : tile_rows + 1, 2 : tile_cols + 2],
    )
    total = jnp.zeros_like(field)
    for direction in range(4):
        index_block = jnp.broadcast_to(tile_links[direction][None], field.shape)
        picked = jnp.take_along_axis(beside[direction], index_block, axis=3)
        total = total - conductance[direction][None] * picked
    return total


def rotate(pair, angle):
    cosine = jnp.cos(angle)
    sine = jnp.sin(angle)
    return jnp.stack([pair[0] * cosine - pair[1] * sine, pair[0] * sine + pair[1] * cosine])


def transform(pair, sign):
    length = pair.shape[1]
    counter = jnp.arange(length)
    product = counter[:, None] * counter[None, :] % length
    angle = 2.0 * math.pi / length * product.astype(jnp.float32)
    cosine = jnp.cos(angle)
    sine = sign * jnp.sin(angle)
    real_in = pair[0]
    imag_in = pair[1]
    out_real = jnp.einsum("kj,j...->k...", cosine, real_in, precision=highest) - jnp.einsum(
        "kj,j...->k...", sine, imag_in, precision=highest
    )
    out_imag = jnp.einsum("kj,j...->k...", cosine, imag_in, precision=highest) + jnp.einsum(
        "kj,j...->k...", sine, real_in, precision=highest
    )
    return jnp.stack([out_real, out_imag])


def on_device(iterate, source, initial, tile_basis, tile_values, capacity, tile_links, conductance):
    local_steps = iterate.shape[0]
    tm_size = lax.axis_size("tm")
    total_steps = local_steps * tm_size
    position = lax.axis_index("tm")
    inner = local_steps // tm_size
    columns = iterate.shape[1] * iterate.shape[2] * iterate.shape[3]
    earlier = from_behind(iterate[-1], "tm", 1)
    earlier = jnp.where(position == 0, initial, earlier)
    previous = jnp.concatenate([earlier[None], iterate[:-1]], axis=0)
    projected = jnp.einsum("rcji,trcj->trci", tile_basis, iterate, precision=highest)
    within = jnp.einsum(
        "rcij,trcj->trci", tile_basis, tile_values[None] * projected, precision=highest
    )
    residual = (
        source
        - capacity[None, :, :, None] * (iterate - previous)
        - within
        - couple(iterate, tile_links, conductance)
    )
    log_alpha = math.log(circulant_alpha)
    step_index = (position * local_steps + jnp.arange(local_steps)).astype(jnp.float32)
    weights = jnp.exp(step_index * (log_alpha / total_steps))[:, None, None, None]
    panel = jnp.stack([residual * weights, jnp.zeros_like(residual)])
    along = jnp.arange(local_steps)
    flat = panel.reshape(2, tm_size, inner, columns)
    mixed = transform(lax.all_to_all(flat, "tm", split_axis=1, concat_axis=1, tiled=True), -1.0)
    global_step = position * inner + jnp.arange(inner)
    freq_low = jnp.arange(tm_size)
    twist_grid = (freq_low[:, None] * global_step[None, :] % total_steps).astype(jnp.float32)
    mixed = rotate(mixed, (-2.0 * math.pi / total_steps * twist_grid)[:, :, None])
    gathered = lax.all_to_all(mixed, "tm", split_axis=1, concat_axis=2, tiled=True)
    spectrum = transform(gathered.reshape(panel.shape), -1.0)
    frequency = (position + tm_size * along).astype(jnp.float32)
    theta = 2.0 * math.pi / total_steps * frequency
    radius = math.exp(log_alpha / total_steps)
    shift_real = capacity[None] * (1.0 - radius * jnp.cos(theta))[:, None, None]
    shift_imag = capacity[None] * (radius * jnp.sin(theta))[:, None, None]
    den_real = tile_values[None] + shift_real[..., None]
    den_imag = jnp.broadcast_to(shift_imag[..., None], den_real.shape)
    magnitude = den_real * den_real + den_imag * den_imag

    def block_solve(pair):
        proj_real = jnp.einsum("rcji,trcj->trci", tile_basis, pair[0], precision=highest)
        proj_imag = jnp.einsum("rcji,trcj->trci", tile_basis, pair[1], precision=highest)
        quot_real = (proj_real * den_real + proj_imag * den_imag) / magnitude
        quot_imag = (proj_imag * den_real - proj_real * den_imag) / magnitude
        out_real = jnp.einsum("rcij,trcj->trci", tile_basis, quot_real, precision=highest)
        out_imag = jnp.einsum("rcij,trcj->trci", tile_basis, quot_imag, precision=highest)
        return jnp.stack([out_real, out_imag])

    first = block_solve(spectrum)
    stacked_shape = (2 * local_steps,) + iterate.shape[1:]
    coupled = couple(first.reshape(stacked_shape), tile_links, conductance).reshape(first.shape)
    second = block_solve(spectrum - coupled)
    backward = transform(second, 1.0) / local_steps
    untwist = 2.0 * math.pi / total_steps * (along * position % total_steps).astype(jnp.float32)
    backward = rotate(backward, untwist[:, None, None, None])
    flat_back = backward.reshape(2, 1, local_steps, columns)
    mixed = (
        transform(lax.all_to_all(flat_back, "tm", split_axis=2, concat_axis=1, tiled=True), 1.0)
        / tm_size
    )
    restored = lax.all_to_all(mixed, "tm", split_axis=1, concat_axis=2, tiled=True).reshape(
        backward.shape
    )
    return iterate + restored[0] / weights


def solution(mesh):
    in_specs = (
        P("tm", "rows", "cols", None),
        P("tm", "rows", "cols", None),
        P("rows", "cols", None),
        P("rows", "cols", None, None),
        P("rows", "cols", None),
        P("rows", "cols"),
        P(None, "rows", "cols", None),
        P(None, "rows", "cols", None),
    )
    out_specs = P("tm", "rows", "cols", None)
    return jax.shard_map(
        on_device, mesh=mesh, in_specs=in_specs, out_specs=out_specs, check_vma=False
    )
```

profile of v0, /device:TPU:2, one launch (start us, length us, event | category | flops | bytes accessed | tf_op | source)
XLA Modules:
  0.0 1013.2 jit_solution(17387815728177091557)
XLA Ops:
  0.0 3.6 collective-permute-start.1
  3.6 3.3 collective-permute-start.2
  6.9 0.8 fusion.260
  7.7 5.1 collective-permute-start.3
  12.8 1.3 collective-permute-start.4
  14.1 0.7 slice_bitcast_fusion.12
  14.8 1.3 collective-permute-start
  16.1 0.7 slice_bitcast_fusion.10
  16.9 0.7 broadcast_add_fusion.3
  17.6 0.7 broadcast_compare_fusion.3
  18.4 0.7 slice_bitcast_fusion.11
  19.2 0.2 fusion.9
  19.7 0.5 copy-done.5
  20.3 73.4 %gather_fusion.2 = f32[8192]{0:T(1024)S(1)} fusion(f32[32,2,128]{2,1,0:T(2,128)S(1)} %get-tuple-element.9, s32[8192]{0:T(1024)S(1)} %bitcast.287), kind=kCustom, calls=%fused_computation.3.clone | custom fusion | bytes 163840 | tf_op jit(solution)/shard_map/jit(take_along_axis)/gather | solution.py:51
  93.8 73.4 %gather_fusion.3 = f32[8192]{0:T(1024)S(1)} fusion(f32[32,2,128]{2,1,0:T(2,128)S(1)} %get-tuple-element.10, s32[8192]{0:T(1024)S(1)} %bitcast.286), kind=kCustom, calls=%fused_computation.4.clone | custom fusion | bytes 163840 | tf_op jit(solution)/shard_map/jit(take_along_axis)/gather | solution.py:51
  167.2 73.4 %gather_fusion = f32[8192]{0:T(1024)S(1)} fusion(f32[32,2,128]{2,1,0:T(2,128)S(1)} %bitcast.278, s32[8192]{0:T(1024)S(1)} %bitcast.284), kind=kCustom, calls=%fused_computation.clone | custom fusion | bytes 163840 | tf_op jit(solution)/shard_map/jit(take_along_axis)/gather | solution.py:51
  240.6 73.4 %gather_fusion.1 = f32[8192]{0:T(1024)S(1)} fusion(f32[32,2,128]{2,1,0:T(2,128)S(1)} %bitcast.279, s32[8192]{0:T(1024)S(1)} %bitcast.285), kind=kCustom, calls=%fused_computation.2.clone | custom fusion | bytes 163840 | tf_op jit(solution)/shard_map/jit(take_along_axis)/gather | solution.py:51
  314.1 0.3 fusion.7
  314.5 0.7 copy.141
  315.1 16.8 %all-to-all-start = ((f32[2,32,1,256]{3,2,0,1:T(1,128)}), f32[2,32,1,256]{3,2,0,1:T(1,128)S(1)}, u32[]{:S(2)}, u32[]{:S(2)}) async-start(f32[2,32,1,256]{3,2,0,1:T(1,128)} %copy.141), calls=%async_computation | async-start | bytes 131072 | tf_op jit(solution)/shard_map/all_to_all | solution.py:106
  332.1 14.3 %all-to-all-done = f32[2,32,1,256]{3,2,0,1:T(1,128)S(1)} async-done(((f32[2,32,1,256]{3,2,0,1:T(1,128)}), f32[2,32,1,256]{3,2,0,1:T(1,128)S(1)}, u32[]{:S(2)}, u32[]{:S(2)}) %all-to-all-start) | async-done | bytes 65568 | tf_op jit(solution)/shard_map/all_to_all | solution.py:106
  346.4 0.2 fusion.89
  346.6 0.2 fusion.93
  346.9 0.2 convolution_add_fusion.3
  347.1 0.2 subtract_bitcast_fusion
  347.4 0.7 copy.142
  348.1 3.8 all-to-all-start.1
  352.0 14.2 %all-to-all-done.1 = f32[2,32,1,256]{3,2,0,1:T(1,128)S(1)} async-done(((f32[2,32,1,256]{3,2,0,1:T(1,128)}), f32[2,32,1,256]{3,2,0,1:T(1,128)S(1)}, u32[]{:S(2)}, u32[]{:S(2)}) %all-to-all-start.1) | async-done | bytes 65568 | tf_op jit(solution)/shard_map/all_to_all | solution.py:111
  366.3 0.2 fusion.125
  366.5 0.2 fusion.121
  366.7 0.2 convolution_subtract_fusion.2
  367.0 0.2 convolution_bitcast_fusion.7
  367.2 0.2 convolution_add_fusion.2
  367.5 0.2 convolution_bitcast_fusion.6
  367.7 0.4 convolution_bitcast_fusion.5
  368.0 0.4 convolution_bitcast_fusion.4
  368.5 1.9 collective-permute-start.5
  370.5 4.8 collective-permute-start.6
  375.3 6.0 collective-permute-start.7
  381.4 1.3 collective-permute-start.8
  382.8 0.2 collective-permute-done.7
  383.0 5.7 collective-permute-done.8
  388.7 0.1 fusion.41
  388.8 146.3 %gather_fusion.6 = f32[16384]{0:T(1024)S(1)} fusion(f32[64,2,128]{2,1,0:T(2,128)S(1)} %get-tuple-element.6, s32[16384]{0:T(1024)S(1)} %bitcast.283), kind=kCustom, calls=%fused_computation.6.clone | custom fusion | bytes 327680 | tf_op jit(solution)/shard_map/jit(take_along_axis)/gather | solution.py:51
  535.2 146.3 %gather_fusion.7 = f32[16384]{0:T(1024)S(1)} fusion(f32[64,2,128]{2,1,0:T(2,128)S(1)} %get-tuple-element.8, s32[16384]{0:T(1024)S(1)} %bitcast.282), kind=kCustom, calls=%fused_computation.7.clone | custom fusion | bytes 327680 | tf_op jit(solution)/shard_map/jit(take_along_axis)/gather | solution.py:51
  681.5 146.3 %gather_fusion.4 = f32[16384]{0:T(1024)S(1)} fusion(f32[64,2,128]{2,1,0:T(2,128)S(1)} %bitcast.276, s32[16384]{0:T(1024)S(1)} %bitcast.280), kind=kCustom, calls=%fused_computation.1.clone | custom fusion | bytes 327680 | tf_op jit(solution)/shard_map/jit(take_along_axis)/gather | solution.py:51
  827.8 146.3 %gather_fusion.5 = f32[16384]{0:T(1024)S(1)} fusion(f32[64,2,128]{2,1,0:T(2,128)S(1)} %bitcast.277, s32[16384]{0:T(1024)S(1)} %bitcast.281), kind=kCustom, calls=%fused_computation.5.clone | custom fusion | bytes 327680 | tf_op jit(solution)/shard_map/jit(take_along_axis)/gather | solution.py:51
  974.2 0.2 fusion.39
  974.3 0.2 convolution_bitcast_fusion.2
  974.5 0.2 convolution_bitcast_fusion.3
  974.8 0.4 convolution_bitcast_fusion.1
  975.1 0.4 convolution_bitcast_fusion
  975.5 0.3 fusion.136
  975.8 0.2 fusion.134
  976.0 0.2 fusion.3
  976.2 0.2 fusion.2
  976.5 0.1 multiply_subtract_fusion
  976.8 17.3 %all_to_all.32 = f32[2,1,32,256]{3,1,0,2:T(1,128)S(1)} all-to-all(f32[2,1,32,256]{3,1,0,2:T(1,128)S(1)} %copy.157), channel_id=1, replica_groups=mesh['tm'=32,'rows'=8,'cols'=2] {'tm'}, dimensions={2} | all-to-all | bytes 131072 | tf_op jit(solution)/shard_map/all_to_all | solution.py:140
  994.1 0.2 fusion.87
  994.3 0.2 fusion.83
  994.6 0.2 fusion.1
  994.8 0.2 fusion
  995.1 17.3 %all_to_all.33 = f32[2,32,1,256]{3,2,0,1:T(1,128)S(1)} all-to-all(f32[2,32,1,256]{3,2,0,1:T(1,128)S(1)} %copy.158), channel_id=1, replica_groups=mesh['tm'=32,'rows'=8,'cols'=2] {'tm'}, dimensions={1} | all-to-all | bytes 131072 | tf_op jit(solution)/shard_map/all_to_all | solution.py:143
  1012.5 0.6 copy.161
  (59 shorter events, 1.3 us)
Async XLA Ops:
  0.0 19.2 %copy-start = (f32[1,2,128,128]{3,2,1,0:T(8,128)S(1)}, f32[1,2,128,128]{3,2,1,0:T(8,128)}, u32[]{:S(2)}) copy-start(f32[1,2,128,128]{3,2,1,0:T(8,128)} %param.15) | copy-start | bytes 393220
  0.0 19.2 %copy-start.1 = (f32[32,1,2,128]{3,2,1,0:T(2,128)S(1)}, f32[32,1,2,128]{3,2,1,0:T(2,128)}, u32[]{:S(2)}) copy-start(f32[32,1,2,128]{3,2,1,0:T(2,128)} %param.12) | copy-start | bytes 98308
  0.0 19.2 %copy-start.3 = (f32[1,2,128]{2,1,0:T(2,128)S(1)}, f32[1,2,128]{2,1,0:T(2,128)}, u32[]{:S(2)}) copy-start(f32[1,2,128]{2,1,0:T(2,128)} %param.16) | copy-start | bytes 3076
  0.0 20.2 %collective-permute-start.1 = (f32[32,1,2,128]{3,2,0,1:T(2,128)}, f32[32,1,2,128]{3,2,0,1:T(2,128)S(1)}, u32[]{:S(2)}, u32[]{:S(2)}) collective-permute-start(f32[32,1,2,128]{3,2,0,1:T(2,128)} %bitcast.288), channel_id=1, source_target_pairs={{0,2},{2,4},{4,6},{6,8},{8,10},{10,12},{12,14},{1,3},{3,5},{5,7},{... | collective-permute-start | bytes 98312 | tf_op jit(solution)/shard_map/ppermute | solution.py:20
  3.6 16.6 %collective-permute-start.2 = (f32[32,1,2,128]{3,2,0,1:T(2,128)}, f32[32,1,2,128]{3,2,0,1:T(2,128)S(1)}, u32[]{:S(2)}, u32[]{:S(2)}) collective-permute-start(f32[32,1,2,128]{3,2,0,1:T(2,128)} %bitcast.289), channel_id=1, source_target_pairs={{2,0},{4,2},{6,4},{8,6},{10,8},{12,10},{14,12},{3,1},{5,3},{7,5},{... | collective-permute-start | bytes 98312 | tf_op jit(solution)/shard_map/ppermute | solution.py:21
  7.7 12.5 %collective-permute-start.3 = (f32[32,1,1,128]{3,2,0,1:T(1,128)S(1)}, f32[32,1,1,128]{3,2,0,1:T(1,128)S(1)}, u32[]{:S(2)}, u32[]{:S(2)}) collective-permute-start(f32[32,1,1,128]{3,2,0,1:T(1,128)S(1)} %get-tuple-element.23), channel_id=1, source_target_pairs={{0,1},{2,3},{4,5},{6,7},{8,9},{10,11},{12,13},{14,15},{16,17},{18,... | collective-permute-start | bytes 49160 | tf_op jit(solution)/shard_map/ppermute | solution.py:20
  12.8 7.4 collective-permute-start.4
  14.8 4.9 collective-permute-start
  16.9 2.6 copy-start.4
  19.5 0.7 copy-start.5
  240.6 73.4 %copy-start.2 = (f32[32,1,2,128]{3,2,1,0:T(2,128)S(1)}, f32[32,1,2,128]{3,2,1,0:T(2,128)}, u32[]{:S(2)}) copy-start(f32[32,1,2,128]{3,2,1,0:T(2,128)} %param.13) | copy-start | bytes 98308
  315.1 31.2 %all-to-all-start = ((f32[2,32,1,256]{3,2,0,1:T(1,128)}), f32[2,32,1,256]{3,2,0,1:T(1,128)S(1)}, u32[]{:S(2)}, u32[]{:S(2)}) async-start(f32[2,32,1,256]{3,2,0,1:T(1,128)} %copy.141), calls=%async_computation | async-start | bytes 131072 | tf_op jit(solution)/shard_map/all_to_all | solution.py:106
  348.1 18.2 %all-to-all-start.1 = ((f32[2,32,1,256]{3,2,0,1:T(1,128)}), f32[2,32,1,256]{3,2,0,1:T(1,128)S(1)}, u32[]{:S(2)}, u32[]{:S(2)}) async-start(f32[2,32,1,256]{3,2,0,1:T(1,128)} %copy.142), calls=%async_computation.1 | async-start | bytes 131072 | tf_op jit(solution)/shard_map/all_to_all | solution.py:111
  368.5 14.2 %collective-permute-start.5 = (f32[64,1,2,128]{3,2,0,1:T(2,128)S(1)}, f32[64,1,2,128]{3,2,0,1:T(2,128)S(1)}, u32[]{:S(2)}, u32[]{:S(2)}) collective-permute-start(f32[64,1,2,128]{3,2,0,1:T(2,128)S(1)} %copy.148), channel_id=1, source_target_pairs={{0,2},{2,4},{4,6},{6,8},{8,10},{10,12},{12,14},{1,3},{3,5},{5,7},{... | collective-permute-start | bytes 196616 | tf_op jit(solution)/shard_map/ppermute | solution.py:20
  370.5 12.3 %collective-permute-start.6 = (f32[64,1,2,128]{3,2,0,1:T(2,128)S(1)}, f32[64,1,2,128]{3,2,0,1:T(2,128)S(1)}, u32[]{:S(2)}, u32[]{:S(2)}) collective-permute-start(f32[64,1,2,128]{3,2,0,1:T(2,128)S(1)} %copy.148), channel_id=1, source_target_pairs={{2,0},{4,2},{6,4},{8,6},{10,8},{12,10},{14,12},{3,1},{5,3},{7,5},{... | collective-permute-start | bytes 196616 | tf_op jit(solution)/shard_map/ppermute | solution.py:21
  375.3 7.6 collective-permute-start.7
  381.4 7.3 collective-permute-start.8
where the time goes:
time: 1010 us
  local copies, waits for them, and re-layouts  885 us (88%)
  starting transfers between devices  49.3 us (5%)
  blocking collectives  34.6 us (3%)
  waiting for transfers between devices  34.4 us (3%)
    gather x12, local copies, waits for them, and re-layouts, couple(): picked = jnp.take_along_axis(beside[direction], index_block, axis=3)  879 us
  transfers between devices with their start and end apart: 11, of which 4 were waited for; matrix products, arithmetic and copies ran while one was open for 1% of the time, Pallas kernels for 0%

commit v1 on v0

v1 whole, which is shorter than its diff:
```python
import math

import jax
import jax.numpy as jnp
from jax import lax
from jax.experimental import pallas as pl
from jax.experimental.pallas import tpu as pltpu
from jax.sharding import PartitionSpec as P

ALPHA = 0.05
HIGHEST = lax.Precision.HIGHEST
STEPS = 32
BLOCKS = 32
TILE = 128
PACK = 40
VECS = 9
f32 = jnp.float32


def mm(x, y):
    return jnp.dot(x, y, precision=HIGHEST, preferred_element_type=f32)


def mm_nt(x, y):
    return lax.dot_general(x, y, (((1,), (1,)), ((), ())), precision=HIGHEST, preferred_element_type=f32)


def mm_tn(x, y):
    return lax.dot_general(x, y, (((0,), (0,)), ((), ())), precision=HIGHEST, preferred_element_type=f32)


def rows_of(shape):
    return lax.broadcasted_iota(jnp.int32, shape, 0)


def shift_down(x, by):
    return jnp.where(rows_of(x.shape) >= by, pltpu.roll(x, by, 0), 0.0)


def recurrence(x, decay):
    for by in (1, 2, 4, 8, 16):
        x = x + decay * shift_down(x, by)
        decay = decay * decay
    return x


def power_rows(decay, first, reverse=False):
    n = rows_of((STEPS, TILE))
    exponent = (STEPS - 1 - n if reverse else n) + first
    out = jnp.ones((STEPS, TILE), f32)
    for bit in range(6):
        out = out * jnp.where((exponent >> bit) & 1 == 1, decay, 1.0)
        decay = decay * decay
    return out


def to_32(decay):
    for _ in range(5):
        decay = decay * decay
    return decay


def picked(x, index_row):
    return jnp.take_along_axis(x, jnp.broadcast_to(index_row, x.shape), axis=1, mode="promise_in_bounds")


def params(values_ref, cap_ref, p):
    total = values_ref[p : p + 1, :] + cap_ref[0, p]
    gain = 1.0 / total
    return cap_ref[0, p] * gain, gain


def coupled(p, low, high, own, side, links_ref, cond_ref, col):
    left = jnp.where(col == 1, side[1], 0.0) if p == 0 else own[0]
    right = own[1] if p == 0 else jnp.where(col == 0, side[0], 0.0)
    total = None
    for d, x in enumerate((low[p], high[p], left, right)):
        r = 2 * d + p
        term = cond_ref[r : r + 1, :] * picked(x, links_ref[r : r + 1, :])
        total = term if total is None else total + term
    return total


def every_other(ref, p, start=0):
    return ref[pl.ds(start + p, STEPS, stride=2), :]


def kernel_a(it, src, low, high, side, bas, values, links, cond, init, cap, out):
    col = lax.axis_index("cols")
    block = lax.axis_index("tm")
    pair = lambda ref: (every_other(ref, 0), every_other(ref, 1))
    lows, highs, sides, own = pair(low), pair(high), pair(side), pair(it)
    for p in range(2):
        basis = bas[p * TILE : (p + 1) * TILE, :]
        decay, gain = params(values, cap, p)
        force = every_other(src, p) + coupled(p, lows, highs, own, sides, links, cond, col)
        last = init[p : p + 1, :] - ALPHA * own[p][STEPS - 1 : STEPS, :]
        stacked = jnp.concatenate([force, jnp.broadcast_to(last, (8, TILE))], axis=0)
        modes = mm(stacked, basis)
        wrap = modes[STEPS : STEPS + 1, :]
        state = recurrence(modes[:STEPS] * gain, decay)
        end = state[STEPS - 1 : STEPS, :]
        end = jnp.where(block == BLOCKS - 1, ALPHA * end + wrap, end)
        row = rows_of((8, TILE))
        tail = jnp.where(row == 0, end, jnp.where(row == 1, decay, jnp.where(row == 2, wrap, 0.0)))
        out[p * PACK : p * PACK + STEPS, :] = mm_nt(state, basis)
        out[p * PACK + STEPS : (p + 1) * PACK, :] = tail


def kernel_b(src, own, low, high, side, bas, values, links, cond, cap, local, send):
    col = lax.axis_index("cols")
    block = lax.axis_index("tm")
    pair = lambda ref: (ref[0:STEPS, :], ref[PACK : PACK + STEPS, :])
    lows, highs, sides, owns = pair(low), pair(high), pair(side), pair(own)
    vectors = [ref[p * PACK + STEPS : p * PACK + STEPS + 1, :] for ref in (own, low, high) for p in range(2)]
    ends = [side[p * PACK + STEPS : p * PACK + STEPS + 1, :] for p in range(2)]
    vectors.append(jnp.where(col == 0, ends[0], ends[1]))
    for p in range(2):
        basis = bas[p * TILE : (p + 1) * TILE, :]
        decay, gain = params(values, cap, p)
        force = every_other(src, p) + coupled(p, lows, highs, owns, sides, links, cond, col)
        state = recurrence(mm(force, basis) * gain, decay)
        local[p * STEPS : (p + 1) * STEPS, :] = state
        end = state[STEPS - 1 : STEPS, :]
        wrap = own[p * PACK + STEPS + 2 : p * PACK + STEPS + 3, :]
        vectors.append(jnp.where(block == BLOCKS - 1, ALPHA * end + wrap, end))
    for k, vector in enumerate(vectors):
        send[pl.ds(k, BLOCKS, stride=VECS), :] = jnp.broadcast_to(vector, (BLOCKS, TILE))


def kernel_m(bas, low, high, side, own2, low2, high2, side2, values, links, cond, cap, direct, through, decays):
    col = lax.axis_index("cols")
    at = lambda ref, p: ref[p * PACK + STEPS + 1 : p * PACK + STEPS + 2, :]
    base = lambda ref, p: ref[2 * STEPS + p * TILE : 2 * STEPS + (p + 1) * TILE, :]
    side_decay = jnp.where(col == 0, at(side2, 0), at(side2, 1))
    side_basis = jnp.where(col == 0, base(side, 0), base(side, 1))
    rows = [at(own2, 0), at(own2, 1), at(low2, 0), at(low2, 1), at(high2, 0), at(high2, 1), side_decay, side_decay]
    for k, row in enumerate(rows):
        decays[k : k + 1, :] = row
    table = [power_rows(row, 1) for row in rows[:7]]
    node = rows_of((TILE, TILE))
    for p in range(2):
        basis = bas[p * TILE : (p + 1) * TILE, :]
        decay, gain = params(values, cap, p)
        own_table = power_rows(decay, 0, reverse=True) * gain
        outside = jnp.where(col == (1 if p == 0 else 0), 1.0, 0.0)
        other = bas[(1 - p) * TILE : (2 - p) * TILE, :]
        slots = [(base(low, p), table[2 + p], None), (base(high, p), table[4 + p], None)]
        inner, outer = (other, table[1 - p], None), (side_basis, table[6], outside)
        slots += [outer, inner] if p == 0 else [inner, outer]
        for d, (neighbour, its_table, mask) in enumerate(slots):
            r = 2 * d + p
            weight = cond[r : r + 1, :] if mask is None else cond[r : r + 1, :] * mask
            ties = jnp.where(links[r : r + 1, :] == node, weight, 0.0)
            matrix = mm_tn(neighbour, mm(ties, basis))
            at_row = (p * 4 + d) * TILE
            direct[at_row : at_row + TILE, :] = matrix
            through[at_row : at_row + TILE, :] = matrix * mm_tn(its_table, own_table)


def incoming(ends, decay):
    block_decay = to_32(decay)
    summed = recurrence(ends, block_decay)
    start = (ALPHA * block_decay * summed[BLOCKS - 2 : BLOCKS - 1, :] + ends[BLOCKS - 1 : BLOCKS, :]) / (
        1.0 - ALPHA * to_32(block_decay)
    )
    return shift_down(summed, 1) + power_rows(block_decay, 0) * start


def row_at(x, index):
    return jnp.sum(jnp.where(rows_of(x.shape) == index, x, 0.0), axis=0, keepdims=True)


def kernel_c(received, local, direct, through, decays, bas, values, cap, out):
    block = lax.axis_index("tm")
    vector = lambda k: received[pl.ds(k, BLOCKS, stride=VECS), :]
    states, paths = [], []
    for k in range(7):
        decay = decays[k : k + 1, :]
        state = incoming(vector(k), decay)
        states.append(state)
        paths.append(power_rows(decay, 1) * row_at(state, block))
    factor = jnp.where(rows_of((BLOCKS, TILE)) == BLOCKS - 1, ALPHA, 1.0)
    for p in range(2):
        order = (2, 4, 6, 1) if p == 0 else (3, 5, 0, 6)
        basis = bas[p * TILE : (p + 1) * TILE, :]
        decay, gain = params(values, cap, p)
        span = slice(p * 4 * TILE, (p + 1) * 4 * TILE)
        added = mm(jnp.concatenate([states[k] for k in order], axis=1), through[span, :])
        ends = vector(7 + p) + factor * added
        entering = row_at(incoming(ends, decay), block)
        force = mm(jnp.concatenate([paths[k] for k in order], axis=1), direct[span, :])
        state = local[p * STEPS : (p + 1) * STEPS, :] + recurrence(force * gain, decay)
        state = state + power_rows(decay, 1) * entering
        out[pl.ds(p, STEPS, stride=2), :] = mm_nt(state, basis)


def call(kernel, outs, *args):
    vmem = pl.BlockSpec(memory_space=pltpu.VMEM)
    smem = pl.BlockSpec(memory_space=pltpu.SMEM)
    shapes = [jax.ShapeDtypeStruct(shape, f32) for shape in outs]
    single = len(outs) == 1
    return pl.pallas_call(
        kernel,
        out_shape=shapes[0] if single else shapes,
        in_specs=[smem if arg.shape == (1, 2) else vmem for arg in args],
        out_specs=vmem if single else [vmem] * len(outs),
    )(*args)


def around(x):
    count = lax.axis_size("rows")
    up = [(i, i + 1) for i in range(count - 1)]
    low = lax.ppermute(x, "rows", up)
    high = lax.ppermute(x, "rows", [(b, a) for a, b in up])
    side = lax.ppermute(x, "cols", [(0, 1), (1, 0)])
    return low, high, side


def on_device(iterate, source, initial, tile_basis, tile_values, capacity, tile_links, conductance):
    it = iterate.reshape(2 * STEPS, TILE)
    src = source.reshape(2 * STEPS, TILE)
    init = initial.reshape(2, TILE)
    bas = tile_basis.reshape(2 * TILE, TILE)
    values = tile_values.reshape(2, TILE)
    links = tile_links.reshape(8, TILE)
    cond = conductance.reshape(8, TILE)
    first = around(jnp.concatenate([it, bas], axis=0))
    own2 = call(kernel_a, [(2 * PACK, TILE)], it, src, *first, bas, values, links, cond, init, capacity)
    second = around(own2)
    local, send = call(
        kernel_b, [(2 * STEPS, TILE), (BLOCKS * VECS, TILE)], src, own2, *second, bas, values, links, cond, capacity
    )
    direct, through, decays = call(
        kernel_m,
        [(8 * TILE, TILE), (8 * TILE, TILE), (8, TILE)],
        bas, *first, own2, *second, values, links, cond, capacity,
    )
    flat = send.reshape(BLOCKS, VECS * TILE)
    received = lax.all_to_all(flat, "tm", split_axis=0, concat_axis=0, tiled=True).reshape(BLOCKS * VECS, TILE)
    out = call(kernel_c, [(2 * STEPS, TILE)], received, local, direct, through, decays, bas, values, capacity)
    return out.reshape(iterate.shape)


def solution(mesh):
    in_specs = (
        P("tm", "rows", "cols", None),
        P("tm", "rows", "cols", None),
        P("rows", "cols", None),
        P("rows", "cols", None, None),
        P("rows", "cols", None),
        P("rows", "cols"),
        P(None, "rows", "cols", None),
        P(None, "rows", "cols", None),
    )
    out_specs = P("tm", "rows", "cols", None)
    return jax.shard_map(on_device, mesh=mesh, in_specs=in_specs, out_specs=out_specs, check_vma=False)
```

time: 1010 us -> 76.7 us (0.08)
  local copies, waits for them, and re-layouts: 885 us -> 1.96 us
  blocking collectives: 34.6 us -> 0 us
  Pallas kernels: 0 us -> 12.7 us
  starting transfers between devices: 49.3 us -> 36.7 us
  waiting for transfers between devices: 34.4 us -> 24 us
    gather x12 -> x0, local copies, waits for them, and re-layouts: 879 us -> none  [couple(): picked = jnp.take_along_axis(beside[direction], index_block, axis=3)]
    all_to_all x2 -> x0, blocking collectives: 34.6 us -> none  [the longest x1 17.3 us: on_device(): lax.all_to_all(flat_back, 'tm', split_axis=2, concat_axis=1, tiled=True)]
    all_to_all x2 -> x1, waiting for transfers between devices: 28.5 us -> 12.9 us  [on_device(): lax.all_to_all(flat, 'tm', split_axis=0, concat_axis=0, tiled=True)]
    pallas_call x0 -> x4, Pallas kernels: none -> 12.7 us  [call(): pl.pallas_call(kernel, out_shape=shapes[0] if single else shapes, in_spec...]
    ppermute x9 -> x6, starting transfers between devices: 28.6 us -> 21.2 us  [the longest x2 7.75 us: around(): high = lax.ppermute(x, 'rows', [(b, a) for a, b in up])]
    all_to_all x2 -> x1, starting transfers between devices: 20.7 us -> 15.5 us  [on_device(): lax.all_to_all(flat, 'tm', split_axis=0, concat_axis=0, tiled=True)]
  transfers between devices with their start and end apart: 11 -> 7, of which waited for: 4 -> 4; matrix products, arithmetic and copies ran while one was open for 1% -> 0% of each run, Pallas kernels for 0% -> 7%
where the time goes in v1:
time: 76.7 us; the launch traced here: 76.3 us
  starting transfers between devices  36.7 us (48%)
  waiting for transfers between devices  24 us (31%)
  Pallas kernels  12.7 us (17%)
  local copies, waits for them, and re-layouts  1.96 us (3%)
  other arithmetic  0.92 us (1%)
    all_to_all x1, starting transfers between devices, on_device(): lax.all_to_all(flat, 'tm', split_axis=0, concat_axis=0, tiled=True)  15.5 us
    all_to_all x1, waiting for transfers between devices, on_device(): lax.all_to_all(flat, 'tm', split_axis=0, concat_axis=0, tiled=True)  12.9 us
    pallas_call x4, Pallas kernels, call(): pl.pallas_call(kernel, out_shape=shapes[0] if single else shapes, in_spec...  12.7 us
    ppermute x2, waiting for transfers between devices, around(): side = lax.ppermute(x, 'cols', [(0, 1), (1, 0)])  10.5 us
    ppermute x2, starting transfers between devices, around(): high = lax.ppermute(x, 'rows', [(b, a) for a, b in up])  7.75 us
    ppermute x2, starting transfers between devices, around(): side = lax.ppermute(x, 'cols', [(0, 1), (1, 0)])  7.74 us
    ppermute x2, starting transfers between devices, around(): low = lax.ppermute(x, 'rows', up)  5.72 us
    unnamed x14, local copies, waits for them, and re-layouts  1.96 us
  transfers between devices with their start and end apart: 7, of which 4 were waited for; matrix products, arithmetic and copies ran while one was open for 0% of the time, Pallas kernels for 7%

profile of v1, /device:TPU:2, one launch (start us, length us, event | category | flops | bytes accessed | tf_op | source)
XLA Modules:
  0.0 76.3 jit_solution(1059328059704467653)
XLA Ops:
  0.0 0.9 %pad_maximum_fusion = f32[320,128]{1,0:T(8,128)S(1)} fusion(f32[256,128]{1,0:T(8,128)} %bitcast.12, f32[64,128]{1,0:T(8,128)} %bitcast.19), kind=kLoop, calls=%fused_computation | loop fusion | flops 40960 | bytes 327680 | tf_op jit(solution)/shard_map/concatenate | solution.py:228
  0.9 3.5 %collective-permute-start = (f32[320,128]{1,0:T(8,128)S(1)}, f32[320,128]{1,0:T(8,128)S(1)}, u32[]{:S(2)}, u32[]{:S(2)}) collective-permute-start(f32[320,128]{1,0:T(8,128)S(1)} %pad_maximum_fusion), channel_id=1, source_target_pairs={{0,2},{2,4},{4,6},{6,8},{8,10},{10,12},{12,14},{1,3},{3,5},{5,7},{... | collective-permute-start | bytes 491528 | tf_op jit(solution)/shard_map/ppermute | solution.py:214
  4.4 3.3 %collective-permute-start.1 = (f32[320,128]{1,0:T(8,128)S(1)}, f32[320,128]{1,0:T(8,128)S(1)}, u32[]{:S(2)}, u32[]{:S(2)}) collective-permute-start(f32[320,128]{1,0:T(8,128)S(1)} %pad_maximum_fusion), channel_id=1, source_target_pairs={{2,0},{4,2},{6,4},{8,6},{10,8},{12,10},{14,12},{3,1},{5,3},{7,5},{... | collective-permute-start | bytes 491528 | tf_op jit(solution)/shard_map/ppermute | solution.py:215
  7.7 5.1 %collective-permute-start.2 = (f32[320,128]{1,0:T(8,128)S(1)}, f32[320,128]{1,0:T(8,128)S(1)}, u32[]{:S(2)}, u32[]{:S(2)}) collective-permute-start(f32[320,128]{1,0:T(8,128)S(1)} %pad_maximum_fusion), channel_id=1, source_target_pairs={{0,1},{1,0},{2,3},{3,2},{4,5},{5,4},{6,7},{7,6},{8,9},{9,8},{10,11... | collective-permute-start | bytes 491528 | tf_op jit(solution)/shard_map/ppermute | solution.py:216
  12.8 0.0 collective-permute-done.low
  12.8 0.0 copy-start
  12.8 0.6 collective-permute-done.1.high
  13.4 0.0 copy-start.1
  13.4 5.5 %collective-permute-done.2.side = f32[320,128]{1,0:T(8,128)S(1)} collective-permute-done((f32[320,128]{1,0:T(8,128)S(1)}, f32[320,128]{1,0:T(8,128)S(1)}, u32[]{:S(2)}, u32[]{:S(2)}) %collective-permute-start.2) | collective-permute-done | bytes 163872 | tf_op jit(solution)/shard_map/ppermute | solution.py:216
  18.9 0.0 copy-start.2
  18.9 0.0 copy-done
  18.9 0.0 copy-done.1
  18.9 0.7 copy-done.2
  19.6 2.5 %shard_map.82.own.own2 = f32[80,128]{1,0:T(8,128)} custom-call(f32[64,128]{1,0:T(8,128)} %bitcast.20, f32[64,128]{1,0:T(8,128)} %bitcast.21, f32[320,128]{1,0:T(8,128)} %copy-done, f32[320,128]{1,0:T(8,128)} %copy-done.1, f32[320,128]{1,0:T(8,128)} %copy-done.2, f32[256,128]{1,0:T(8,128)} %bitcast.13, f32[2,128]{1,0:T(2,128)} %bitcast.29, ...), custom_call_target="tpu_custom_call" | custom-call | tf_op jit(solution)/shard_map/pallas_call | solution.py:203
  22.1 2.2 %collective-permute-start.3 = (f32[80,128]{1,0:T(8,128)}, f32[80,128]{1,0:T(8,128)S(1)}, u32[]{:S(2)}, u32[]{:S(2)}) collective-permute-start(f32[80,128]{1,0:T(8,128)} %shard_map.82.own.own2), channel_id=1, source_target_pairs={{0,2},{2,4},{4,6},{6,8},{8,10},{10,12},{12,14},{1,3},{3,5},{5,7},{... | collective-permute-start | bytes 122888 | tf_op jit(solution)/shard_map/ppermute | solution.py:214
  24.4 4.5 %collective-permute-start.4 = (f32[80,128]{1,0:T(8,128)}, f32[80,128]{1,0:T(8,128)S(1)}, u32[]{:S(2)}, u32[]{:S(2)}) collective-permute-start(f32[80,128]{1,0:T(8,128)} %shard_map.82.own.own2), channel_id=1, source_target_pairs={{2,0},{4,2},{6,4},{8,6},{10,8},{12,10},{14,12},{3,1},{5,3},{7,5},{... | collective-permute-start | bytes 122888 | tf_op jit(solution)/shard_map/ppermute | solution.py:215
  28.9 2.6 %collective-permute-start.5 = (f32[80,128]{1,0:T(8,128)}, f32[80,128]{1,0:T(8,128)S(1)}, u32[]{:S(2)}, u32[]{:S(2)}) collective-permute-start(f32[80,128]{1,0:T(8,128)} %shard_map.82.own.own2), channel_id=1, source_target_pairs={{0,1},{1,0},{2,3},{3,2},{4,5},{5,4},{6,7},{7,6},{8,9},{9,8},{10,11... | collective-permute-start | bytes 122888 | tf_op jit(solution)/shard_map/ppermute | solution.py:216
  31.5 0.0 collective-permute-done.3.low.low2
  31.5 0.0 copy-start.4
  31.5 0.0 collective-permute-done.4.high.high2
  31.6 0.0 copy-start.5
  31.6 4.9 %collective-permute-done.5.side.side2 = f32[80,128]{1,0:T(8,128)S(1)} collective-permute-done((f32[80,128]{1,0:T(8,128)}, f32[80,128]{1,0:T(8,128)S(1)}, u32[]{:S(2)}, u32[]{:S(2)}) %collective-permute-start.5) | collective-permute-done | bytes 40992 | tf_op jit(solution)/shard_map/ppermute | solution.py:216
  36.5 0.0 copy-done.4
  36.5 0.0 copy-done.5
  36.5 0.0 copy-start.6
  36.5 0.6 copy-done.6
  37.1 2.0 %shard_map.83 = (f32[64,128]{1,0:T(8,128)}, f32[288,128]{1,0:T(8,128)}) custom-call(f32[64,128]{1,0:T(8,128)} %bitcast.22, f32[80,128]{1,0:T(8,128)} %shard_map.82.own.own2, f32[80,128]{1,0:T(8,128)} %copy-done.4, f32[80,128]{1,0:T(8,128)} %copy-done.5, f32[80,128]{1,0:T(8,128)} %copy-done.6, f32[256,128]{1,0:T(8,128)} %bitcast.14, f32[2,128]{1,0:T(2,128)} %bitcast.30, ...), custom_call_target="tpu_custom_call" | custom-call | tf_op jit(solution)/shard_map/pallas_call | solution.py:203
  39.1 15.5 %all-to-all-start = ((f32[32,1,1152]{2,1,0:T(1,128)}), f32[32,1,1152]{2,1,0:T(1,128)S(1)}, u32[]{:S(2)}, u32[]{:S(2)}) async-start(f32[32,1,1152]{2,1,0:T(1,128)} %bitcast.18), calls=%async_computation | async-start | bytes 294912 | tf_op jit(solution)/shard_map/all_to_all | solution.py:240
  54.6 5.0 %shard_map.84 = (f32[1024,128]{1,0:T(8,128)}, f32[1024,128]{1,0:T(8,128)}, f32[8,128]{1,0:T(8,128)}) custom-call(f32[256,128]{1,0:T(8,128)} %bitcast.15, f32[320,128]{1,0:T(8,128)} %copy-done, f32[320,128]{1,0:T(8,128)} %copy-done.1, f32[320,128]{1,0:T(8,128)} %copy-done.2, f32[80,128]{1,0:T(8,128)} %shard_map.82.own.own2, f32[80,128]{1,0:T(8,128)} %copy-done.4, ...), custom_call_target="tpu_custom_call" | custom-call | tf_op jit(solution)/shard_map/pallas_call | solution.py:203
  59.6 12.9 %all-to-all-done = f32[32,1,1152]{2,1,0:T(1,128)S(1)} async-done(((f32[32,1,1152]{2,1,0:T(1,128)}), f32[32,1,1152]{2,1,0:T(1,128)S(1)}, u32[]{:S(2)}, u32[]{:S(2)}) %all-to-all-start) | async-done | bytes 147488 | tf_op jit(solution)/shard_map/all_to_all | solution.py:240
  72.5 0.0 copy-start.3
  72.5 0.7 copy-done.3
  73.2 3.2 %shard_map.85 = f32[64,128]{1,0:T(8,128)} custom-call(f32[288,128]{1,0:T(8,128)} %bitcast.17, f32[64,128]{1,0:T(8,128)} %get-tuple-element.11.local, f32[1024,128]{1,0:T(8,128)} %get-tuple-element.12.direct, f32[1024,128]{1,0:T(8,128)} %get-tuple-element.13.through, f32[8,128]{1,0:T(8,128)} %get-tuple-element.14.decays, f32[256,128]{1,0:T(8,128)} %bitcast.16, ...), custom_call_target="tpu_custom_call" | custom-call | tf_op jit(solution)/shard_map/pallas_call | solution.py:203
Async XLA Ops:
  0.9 11.9 %collective-permute-start = (f32[320,128]{1,0:T(8,128)S(1)}, f32[320,128]{1,0:T(8,128)S(1)}, u32[]{:S(2)}, u32[]{:S(2)}) collective-permute-start(f32[320,128]{1,0:T(8,128)S(1)} %pad_maximum_fusion), channel_id=1, source_target_pairs={{0,2},{2,4},{4,6},{6,8},{8,10},{10,12},{12,14},{1,3},{3,5},{5,7},{... | collective-permute-start | bytes 491528 | tf_op jit(solution)/shard_map/ppermute | solution.py:214
  4.4 9.0 %collective-permute-start.1 = (f32[320,128]{1,0:T(8,128)S(1)}, f32[320,128]{1,0:T(8,128)S(1)}, u32[]{:S(2)}, u32[]{:S(2)}) collective-permute-start(f32[320,128]{1,0:T(8,128)S(1)} %pad_maximum_fusion), channel_id=1, source_target_pairs={{2,0},{4,2},{6,4},{8,6},{10,8},{12,10},{14,12},{3,1},{5,3},{7,5},{... | collective-permute-start | bytes 491528 | tf_op jit(solution)/shard_map/ppermute | solution.py:215
  7.7 11.2 %collective-permute-start.2 = (f32[320,128]{1,0:T(8,128)S(1)}, f32[320,128]{1,0:T(8,128)S(1)}, u32[]{:S(2)}, u32[]{:S(2)}) collective-permute-start(f32[320,128]{1,0:T(8,128)S(1)} %pad_maximum_fusion), channel_id=1, source_target_pairs={{0,1},{1,0},{2,3},{3,2},{4,5},{5,4},{6,7},{7,6},{8,9},{9,8},{10,11... | collective-permute-start | bytes 491528 | tf_op jit(solution)/shard_map/ppermute | solution.py:216
  12.8 6.1 %copy-start = (f32[320,128]{1,0:T(8,128)}, f32[320,128]{1,0:T(8,128)S(1)}, u32[]{:S(2)}) copy-start(f32[320,128]{1,0:T(8,128)S(1)} %collective-permute-done.low) | copy-start | bytes 491524
  13.4 5.6 %copy-start.1 = (f32[320,128]{1,0:T(8,128)}, f32[320,128]{1,0:T(8,128)S(1)}, u32[]{:S(2)}) copy-start(f32[320,128]{1,0:T(8,128)S(1)} %collective-permute-done.1.high) | copy-start | bytes 491524
  18.9 0.7 copy-start.2
  22.1 9.4 %collective-permute-start.3 = (f32[80,128]{1,0:T(8,128)}, f32[80,128]{1,0:T(8,128)S(1)}, u32[]{:S(2)}, u32[]{:S(2)}) collective-permute-start(f32[80,128]{1,0:T(8,128)} %shard_map.82.own.own2), channel_id=1, source_target_pairs={{0,2},{2,4},{4,6},{6,8},{8,10},{10,12},{12,14},{1,3},{3,5},{5,7},{... | collective-permute-start | bytes 122888 | tf_op jit(solution)/shard_map/ppermute | solution.py:214
  24.4 7.2 %collective-permute-start.4 = (f32[80,128]{1,0:T(8,128)}, f32[80,128]{1,0:T(8,128)S(1)}, u32[]{:S(2)}, u32[]{:S(2)}) collective-permute-start(f32[80,128]{1,0:T(8,128)} %shard_map.82.own.own2), channel_id=1, source_target_pairs={{2,0},{4,2},{6,4},{8,6},{10,8},{12,10},{14,12},{3,1},{5,3},{7,5},{... | collective-permute-start | bytes 122888 | tf_op jit(solution)/shard_map/ppermute | solution.py:215
  28.9 7.6 %collective-permute-start.5 = (f32[80,128]{1,0:T(8,128)}, f32[80,128]{1,0:T(8,128)S(1)}, u32[]{:S(2)}, u32[]{:S(2)}) collective-permute-start(f32[80,128]{1,0:T(8,128)} %shard_map.82.own.own2), channel_id=1, source_target_pairs={{0,1},{1,0},{2,3},{3,2},{4,5},{5,4},{6,7},{7,6},{8,9},{9,8},{10,11... | collective-permute-start | bytes 122888 | tf_op jit(solution)/shard_map/ppermute | solution.py:216
  31.5 5.0 %copy-start.4 = (f32[80,128]{1,0:T(8,128)}, f32[80,128]{1,0:T(8,128)S(1)}, u32[]{:S(2)}) copy-start(f32[80,128]{1,0:T(8,128)S(1)} %collective-permute-done.3.low.low2) | copy-start | bytes 122884
  31.6 4.9 %copy-start.5 = (f32[80,128]{1,0:T(8,128)}, f32[80,128]{1,0:T(8,128)S(1)}, u32[]{:S(2)}) copy-start(f32[80,128]{1,0:T(8,128)S(1)} %collective-permute-done.4.high.high2) | copy-start | bytes 122884
  36.5 0.6 copy-start.6
  39.1 33.4 %all-to-all-start = ((f32[32,1,1152]{2,1,0:T(1,128)}), f32[32,1,1152]{2,1,0:T(1,128)S(1)}, u32[]{:S(2)}, u32[]{:S(2)}) async-start(f32[32,1,1152]{2,1,0:T(1,128)} %bitcast.18), calls=%async_computation | async-start | bytes 294912 | tf_op jit(solution)/shard_map/all_to_all | solution.py:240
  72.5 0.7 copy-start.3

commit v2 on v1

--- a/solution.py
+++ b/solution.py
@@ -14,6 +14,9 @@
 TILE = 128
 PACK = 40
 VECS = 9
+FIRST = 22
+TURNED = [(i + FIRST) % BLOCKS for i in range(BLOCKS)]
+ROWS2 = 2 * PACK
 f32 = jnp.float32
 
 
@@ -71,8 +74,8 @@
 
 
 def coupled(p, low, high, own, side, links_ref, cond_ref, col):
-    left = jnp.where(col == 1, side[1], 0.0) if p == 0 else own[0]
-    right = own[1] if p == 0 else jnp.where(col == 0, side[0], 0.0)
+    left = jnp.where(col == 1, side, 0.0) if p == 0 else own[0]
+    right = own[1] if p == 0 else jnp.where(col == 0, side, 0.0)
     total = None
     for d, x in enumerate((low[p], high[p], left, right)):
         r = 2 * d + p
@@ -85,11 +88,25 @@
     return ref[pl.ds(start + p, STEPS, stride=2), :]
 
 
-def kernel_a(it, src, low, high, side, bas, values, links, cond, init, cap, out):
+def kernel_p(it, bas, values, links, cond, init, rows_pack, cols_pack, values_out, links_out, cond_out, init_out):
+    col = lax.axis_index("cols")
+    rows_pack[0 : 2 * STEPS, :] = it[...]
+    rows_pack[2 * STEPS :, :] = bas[...]
+    near = 1 - col
+    cols_pack[0:STEPS, :] = jnp.where(col == 0, every_other(it, 1), every_other(it, 0))
+    cols_pack[STEPS:, :] = bas[pl.ds(pl.multiple_of(near * TILE, TILE), TILE), :]
+    values_out[...] = values[...]
+    links_out[...] = links[...]
+    cond_out[...] = cond[...]
+    init_out[...] = init[...]
+
+
+def kernel_a(it, src, inner, outer, side, bas, values, links, cond, init, cap, out, copies):
     col = lax.axis_index("cols")
     block = lax.axis_index("tm")
     pair = lambda ref: (every_other(ref, 0), every_other(ref, 1))
-    lows, highs, sides, own = pair(low), pair(high), pair(side), pair(it)
+    sides, own = side[0:STEPS, :], pair(it)
+    lows, highs = zip(*(ordered(a, b) for a, b in zip(pair(inner), pair(outer))))
     for p in range(2):
         basis = bas[p * TILE : (p + 1) * TILE, :]
         decay, gain = params(values, cap, p)
@@ -103,18 +120,31 @@
         end = jnp.where(block == BLOCKS - 1, ALPHA * end + wrap, end)
         row = rows_of((8, TILE))
         tail = jnp.where(row == 0, end, jnp.where(row == 1, decay, jnp.where(row == 2, wrap, 0.0)))
-        out[p * PACK : p * PACK + STEPS, :] = mm_nt(state, basis)
-        out[p * PACK + STEPS : (p + 1) * PACK, :] = tail
-
-
-def kernel_b(src, own, low, high, side, bas, values, links, cond, cap, local, send):
+        first = mm_nt(state, basis)
+        for ref, rows in ((out, ROWS2), (copies, 4 * ROWS2)):
+            for at in range(p * PACK, rows, ROWS2):
+                ref[at : at + STEPS, :] = first
+                ref[at + STEPS : at + PACK, :] = tail
+
+
+def quad_rows(start, count):
+    odd, col = lax.axis_index("rows") % 2, lax.axis_index("cols")
+    inner = ((1 - odd) * 2 + col) * ROWS2 + start
+    near = jnp.where(col == 0, 0, PACK)
+    side = (odd * 2 + 1 - col) * ROWS2 + near + start
+    return pl.ds(pl.multiple_of(inner, 8), count), pl.ds(pl.multiple_of(side, 8), count)
+
+
+def kernel_b(src, own, quad, outer, bas, values, links, cond, cap, local, send):
     col = lax.axis_index("cols")
     block = lax.axis_index("tm")
-    pair = lambda ref: (ref[0:STEPS, :], ref[PACK : PACK + STEPS, :])
-    lows, highs, sides, owns = pair(low), pair(high), pair(side), pair(own)
-    vectors = [ref[p * PACK + STEPS : p * PACK + STEPS + 1, :] for ref in (own, low, high) for p in range(2)]
-    ends = [side[p * PACK + STEPS : p * PACK + STEPS + 1, :] for p in range(2)]
-    vectors.append(jnp.where(col == 0, ends[0], ends[1]))
+    both = lambda ref, start, count: [ref[p * PACK + start : p * PACK + start + count, :] for p in range(2)]
+    inner = lambda start, count: [quad[quad_rows(p * PACK + start, count)[0], :] for p in range(2)]
+    side = lambda start, count: quad[quad_rows(start, count)[1], :]
+    owns, sides = both(own, 0, STEPS), side(0, STEPS)
+    lows, highs = zip(*(ordered(a, b) for a, b in zip(inner(0, STEPS), both(outer, 0, STEPS))))
+    low_ends, high_ends = zip(*(ordered(a, b) for a, b in zip(inner(STEPS, 8), both(outer, STEPS, 8))))
+    vectors = [x[0:1, :] for x in (*both(own, STEPS, 8), *low_ends, *high_ends, side(STEPS, 8))]
     for p in range(2):
         basis = bas[p * TILE : (p + 1) * TILE, :]
         decay, gain = params(values, cap, p)
@@ -128,13 +158,15 @@
         send[pl.ds(k, BLOCKS, stride=VECS), :] = jnp.broadcast_to(vector, (BLOCKS, TILE))
 
 
-def kernel_m(bas, low, high, side, own2, low2, high2, side2, values, links, cond, cap, direct, through, decays):
+def kernel_m(bas, inner, outer, side, own2, quad, outer2, values, links, cond, cap, direct, through, decays):
     col = lax.axis_index("cols")
-    at = lambda ref, p: ref[p * PACK + STEPS + 1 : p * PACK + STEPS + 2, :]
+    at = lambda ref, p: ref[p * PACK + STEPS : p * PACK + STEPS + 8, :][1:2, :]
     base = lambda ref, p: ref[2 * STEPS + p * TILE : 2 * STEPS + (p + 1) * TILE, :]
-    side_decay = jnp.where(col == 0, at(side2, 0), at(side2, 1))
-    side_basis = jnp.where(col == 0, base(side, 0), base(side, 1))
-    rows = [at(own2, 0), at(own2, 1), at(low2, 0), at(low2, 1), at(high2, 0), at(high2, 1), side_decay, side_decay]
+    side_decay = quad[quad_rows(STEPS, 8)[1], :][1:2, :]
+    side_basis = side[STEPS : STEPS + TILE, :]
+    inner_decay = [quad[quad_rows(p * PACK + STEPS, 8)[0], :][1:2, :] for p in range(2)]
+    low_decay, high_decay = zip(*(ordered(inner_decay[p], at(outer2, p)) for p in range(2)))
+    rows = [at(own2, 0), at(own2, 1), *low_decay, *high_decay, side_decay, side_decay]
     for k, row in enumerate(rows):
         decays[k : k + 1, :] = row
     table = [power_rows(row, 1) for row in rows[:7]]
@@ -145,9 +177,10 @@
         own_table = power_rows(decay, 0, reverse=True) * gain
         outside = jnp.where(col == (1 if p == 0 else 0), 1.0, 0.0)
         other = bas[(1 - p) * TILE : (2 - p) * TILE, :]
-        slots = [(base(low, p), table[2 + p], None), (base(high, p), table[4 + p], None)]
-        inner, outer = (other, table[1 - p], None), (side_basis, table[6], outside)
-        slots += [outer, inner] if p == 0 else [inner, outer]
+        low, high = ordered(base(inner, p), base(outer, p))
+        slots = [(low, table[2 + p], None), (high, table[4 + p], None)]
+        near, far = (other, table[1 - p], None), (side_basis, table[6], outside)
+        slots += [far, near] if p == 0 else [near, far]
         for d, (neighbour, its_table, mask) in enumerate(slots):
             r = 2 * d + p
             weight = cond[r : r + 1, :] if mask is None else cond[r : r + 1, :] * mask
@@ -173,7 +206,7 @@
 
 def kernel_c(received, local, direct, through, decays, bas, values, cap, out):
     block = lax.axis_index("tm")
-    vector = lambda k: received[pl.ds(k, BLOCKS, stride=VECS), :]
+    vector = lambda k: pltpu.roll(received[pl.ds(k, BLOCKS, stride=VECS), :], FIRST, 0)
     states, paths = [], []
     for k in range(7):
         decay = decays[k : k + 1, :]
@@ -195,26 +228,29 @@
         out[pl.ds(p, STEPS, stride=2), :] = mm_nt(state, basis)
 
 
-def call(kernel, outs, *args):
+def call(kernel, outs, *args, last=False, plain=False):
     vmem = pl.BlockSpec(memory_space=pltpu.VMEM)
     smem = pl.BlockSpec(memory_space=pltpu.SMEM)
-    shapes = [jax.ShapeDtypeStruct(shape, f32) for shape in outs]
+    outs = [out if isinstance(out[0], tuple) else (out, f32) for out in outs]
+    shapes = [jax.ShapeDtypeStruct(*out) if last else pltpu.VMEM(*out) for out in outs]
     single = len(outs) == 1
+    scalar = lambda arg: arg.shape == (1, 2)
+    near = lambda arg: arg if plain or scalar(arg) else pltpu.with_memory_space_constraint(arg, pltpu.VMEM)
     return pl.pallas_call(
         kernel,
         out_shape=shapes[0] if single else shapes,
-        in_specs=[smem if arg.shape == (1, 2) else vmem for arg in args],
+        in_specs=[smem if scalar(arg) else vmem for arg in args],
         out_specs=vmem if single else [vmem] * len(outs),
-    )(*args)
-
-
-def around(x):
-    count = lax.axis_size("rows")
-    up = [(i, i + 1) for i in range(count - 1)]
-    low = lax.ppermute(x, "rows", up)
-    high = lax.ppermute(x, "rows", [(b, a) for a, b in up])
-    side = lax.ppermute(x, "cols", [(0, 1), (1, 0)])
-    return low, high, side
+    )(*[near(arg) for arg in args])
+
+
+def swaps(first):
+    return [pair for i in range(first, lax.axis_size("rows") - 1, 2) for pair in ((i, i + 1), (i + 1, i))]
+
+
+def ordered(inner, outer):
+    odd = lax.axis_index("rows") % 2 == 1
+    return jnp.where(odd, inner, outer), jnp.where(odd, outer, inner)
 
 
 def on_device(iterate, source, initial, tile_basis, tile_values, capacity, tile_links, conductance):
@@ -225,20 +261,36 @@
     values = tile_values.reshape(2, TILE)
     links = tile_links.reshape(8, TILE)
     cond = conductance.reshape(8, TILE)
-    first = around(jnp.concatenate([it, bas], axis=0))
-    own2 = call(kernel_a, [(2 * PACK, TILE)], it, src, *first, bas, values, links, cond, init, capacity)
-    second = around(own2)
+    rows_pack, cols_pack, values, links, cond, init = call(
+        kernel_p,
+        [(2 * STEPS + 2 * TILE, TILE), (STEPS + TILE, TILE), (2, TILE), ((8, TILE), jnp.int32), (8, TILE), (2, TILE)],
+        it, bas, values, links, cond, init, plain=True,
+    )
+    inner = lax.ppermute(rows_pack, "rows", swaps(0))
+    outer = lax.ppermute(rows_pack, "rows", swaps(1))
+    side = lax.ppermute(cols_pack, "cols", [(0, 1), (1, 0)])
+    own2, copies = call(
+        kernel_a, [(ROWS2, TILE), (4 * ROWS2, TILE)], it, src, inner, outer, side, bas, values, links, cond, init, capacity
+    )
+    fours = [[4 * k + j for j in range(4)] for k in range(lax.axis_size("rows") // 2)]
+    quad = lax.all_to_all(
+        copies.reshape(4, ROWS2, TILE), ("rows", "cols"), split_axis=0, concat_axis=0, tiled=True,
+        axis_index_groups=fours,
+    ).reshape(4 * ROWS2, TILE)
+    outer2 = lax.ppermute(own2, "rows", swaps(1))
     local, send = call(
-        kernel_b, [(2 * STEPS, TILE), (BLOCKS * VECS, TILE)], src, own2, *second, bas, values, links, cond, capacity
+        kernel_b, [(2 * STEPS, TILE), (BLOCKS * VECS, TILE)], src, own2, quad, outer2, bas, values, links, cond, capacity
     )
     direct, through, decays = call(
         kernel_m,
         [(8 * TILE, TILE), (8 * TILE, TILE), (8, TILE)],
-        bas, *first, own2, *second, values, links, cond, capacity,
+        bas, inner, outer, side, own2, quad, outer2, values, links, cond, capacity,
     )
     flat = send.reshape(BLOCKS, VECS * TILE)
-    received = lax.all_to_all(flat, "tm", split_axis=0, concat_axis=0, tiled=True).reshape(BLOCKS * VECS, TILE)
-    out = call(kernel_c, [(2 * STEPS, TILE)], received, local, direct, through, decays, bas, values, capacity)
+    received = lax.all_to_all(
+        flat, "tm", split_axis=0, concat_axis=0, tiled=True, axis_index_groups=[TURNED]
+    ).reshape(BLOCKS * VECS, TILE)
+    out = call(kernel_c, [(2 * STEPS, TILE)], received, local, direct, through, decays, bas, values, capacity, last=True)
     return out.reshape(iterate.shape)
 
 

time: 76.7 us -> 60.7 us (0.79)
  the two profiles are of different devices: /device:TPU:2 before, /device:TPU:11 now
where the time goes in v2:
time: 60.7 us; the launch traced here: 60.3 us
  starting transfers between devices  35.8 us (59%)
  waiting for transfers between devices  13.7 us (23%)
  Pallas kernels  10.7 us (18%)
    all_to_all x1, starting transfers between devices, on_device(): lax.all_to_all(flat, 'tm', split_axis=0, concat_axis=0, tiled=True, axis_...  17.4 us
    pallas_call x5, Pallas kernels, call(): pl.pallas_call(kernel, out_shape=shapes[0] if single else shapes, in_spec...  10.7 us
    all_to_all x1, waiting for transfers between devices, on_device(): lax.all_to_all(flat, 'tm', split_axis=0, concat_axis=0, tiled=True, axis_...  6.84 us
    all_to_all x1, starting transfers between devices, on_device(): lax.all_to_all(copies.reshape(4, ROWS2, TILE), ('rows', 'cols'), split_ax...  5.86 us
    ppermute x1, starting transfers between devices, on_device(): outer = lax.ppermute(rows_pack, 'rows', swaps(1))  4.13 us
    ppermute x1, starting transfers between devices, on_device(): side = lax.ppermute(cols_pack, 'cols', [(0, 1), (1, 0)])  3.92 us
    ppermute x1, waiting for transfers between devices, on_device(): side = lax.ppermute(cols_pack, 'cols', [(0, 1), (1, 0)])  3.59 us
    ppermute x1, waiting for transfers between devices, on_device(): outer2 = lax.ppermute(own2, 'rows', swaps(1))  3.28 us
  transfers between devices with their start and end apart: 6, of which 3 were waited for; matrix products, arithmetic and copies ran while one was open for 0% of the time, Pallas kernels for 6%

profile of v2, /device:TPU:11, one launch (start us, length us, event | category | flops | bytes accessed | tf_op | source)
XLA Modules:
  0.0 60.3 jit_solution(16683524397640958661)
XLA Ops:
  0.0 0.0 copy-start
  0.0 0.0 copy-start.1
  0.0 0.0 copy-start.2
  0.0 1.0 %shard_map.82 = (f32[320,128]{1,0:T(8,128)S(1)}, f32[160,128]{1,0:T(8,128)S(1)}, f32[2,128]{1,0:T(2,128)S(1)}, s32[8,128]{1,0:T(8,128)S(1)}, f32[8,128]{1,0:T(8,128)S(1)}, /*index=5*/f32[2,128]{1,0:T(2,128)S(1)}) custom-call(f32[64,128]{1,0:T(8,128)} %bitcast.24, f32[256,128]{1,0:T(8,128)} %bitcast.14, f32[2,128]{1,0:T(2,128)} %bitcast.28, ...), custom_call_target="tpu_custom_call" | custom-call | tf_op jit(solution)/shard_map/pallas_call | solution.py:239
  1.0 2.1 %collective-permute-start = (f32[320,128]{1,0:T(8,128)S(1)}, f32[320,128]{1,0:T(8,128)S(1)}, u32[]{:S(2)}, u32[]{:S(2)}) collective-permute-start(f32[320,128]{1,0:T(8,128)S(1)} %get-tuple-element.18), channel_id=1, source_target_pairs={{0,2},{2,0},{4,6},{6,4},{8,10},{10,8},{12,14},{14,12},{1,3},{3,1},... | collective-permute-start | bytes 491528 | tf_op jit(solution)/shard_map/ppermute | solution.py:269
  3.1 4.1 %collective-permute-start.1 = (f32[320,128]{1,0:T(8,128)S(1)}, f32[320,128]{1,0:T(8,128)S(1)}, u32[]{:S(2)}, u32[]{:S(2)}) collective-permute-start(f32[320,128]{1,0:T(8,128)S(1)} %get-tuple-element.18), channel_id=1, source_target_pairs={{2,4},{4,2},{6,8},{8,6},{10,12},{12,10},{3,5},{5,3},{7,9},{9,7},{1... | collective-permute-start | bytes 491528 | tf_op jit(solution)/shard_map/ppermute | solution.py:270
  7.2 3.9 %collective-permute-start.2 = (f32[160,128]{1,0:T(8,128)S(1)}, f32[160,128]{1,0:T(8,128)S(1)}, u32[]{:S(2)}, u32[]{:S(2)}) collective-permute-start(f32[160,128]{1,0:T(8,128)S(1)} %get-tuple-element.19), channel_id=1, source_target_pairs={{0,1},{1,0},{2,3},{3,2},{4,5},{5,4},{6,7},{7,6},{8,9},{9,8},{10,11... | collective-permute-start | bytes 245768 | tf_op jit(solution)/shard_map/ppermute | solution.py:271
  11.2 3.6 %collective-permute-done.2.side = f32[160,128]{1,0:T(8,128)S(1)} collective-permute-done((f32[160,128]{1,0:T(8,128)S(1)}, f32[160,128]{1,0:T(8,128)S(1)}, u32[]{:S(2)}, u32[]{:S(2)}) %collective-permute-start.2) | collective-permute-done | bytes 81952 | tf_op jit(solution)/shard_map/ppermute | solution.py:271
  14.7 0.0 collective-permute-done.inner
  14.8 0.0 collective-permute-done.1.outer
  14.8 0.0 copy-done
  14.8 0.0 copy-done.1
  14.8 0.0 copy-done.2
  14.8 2.0 %shard_map.83 = (f32[80,128]{1,0:T(8,128)S(1)}, f32[320,128]{1,0:T(8,128)}) custom-call(f32[64,128]{1,0:T(8,128)S(1)} %bitcast.25, f32[64,128]{1,0:T(8,128)S(1)} %bitcast.22, f32[320,128]{1,0:T(8,128)S(1)} %collective-permute-done.inner, f32[320,128]{1,0:T(8,128)S(1)} %collective-permute-done.1.outer, f32[160,128]{1,0:T(8,128)S(1)} %collective-permute-done.2.side, ...), custom_call_target="tpu_custom_call" | custom-call | tf_op jit(solution)/shard_map/pallas_call | solution.py:239
  16.8 5.9 %all-to-all-start = ((f32[4,80,128]{2,1,0:T(8,128)}), f32[4,80,128]{2,1,0:T(8,128)S(1)}, u32[]{:S(2)}, u32[]{:S(2)}) async-start(f32[4,80,128]{2,1,0:T(8,128)} %bitcast.7), calls=%async_computation | async-start | bytes 327680 | tf_op jit(solution)/shard_map/all_to_all | solution.py:276
  22.7 2.4 %collective-permute-start.3 = (f32[80,128]{1,0:T(8,128)S(1)}, f32[80,128]{1,0:T(8,128)S(1)}, u32[]{:S(2)}, u32[]{:S(2)}) collective-permute-start(f32[80,128]{1,0:T(8,128)S(1)} %get-tuple-element.24.own.own2), channel_id=1, source_target_pairs={{2,4},{4,2},{6,8},{8,6},{10,12},{12,10},{3,5},{5,3},{7,9},{9,7},{1... | collective-permute-start | bytes 122888 | tf_op jit(solution)/shard_map/ppermute | solution.py:280
  25.1 3.3 %collective-permute-done.3.outer.outer2 = f32[80,128]{1,0:T(8,128)S(1)} collective-permute-done((f32[80,128]{1,0:T(8,128)S(1)}, f32[80,128]{1,0:T(8,128)S(1)}, u32[]{:S(2)}, u32[]{:S(2)}) %collective-permute-start.3) | collective-permute-done | bytes 40992 | tf_op jit(solution)/shard_map/ppermute | solution.py:280
  28.4 0.0 all-to-all-done
  28.4 1.7 %shard_map.84 = (f32[64,128]{1,0:T(8,128)S(1)}, f32[288,128]{1,0:T(8,128)}) custom-call(f32[64,128]{1,0:T(8,128)S(1)} %bitcast.23, f32[80,128]{1,0:T(8,128)S(1)} %get-tuple-element.24.own.own2, f32[320,128]{1,0:T(8,128)S(1)} %bitcast.19, f32[80,128]{1,0:T(8,128)S(1)} %collective-permute-done.3.outer.outer2, f32[256,128]{1,0:T(8,128)S(1)} %bitcast.16, ...), custom_call_target="tpu_custom_call" | custom-call | tf_op jit(solution)/shard_map/pallas_call | solution.py:239
  30.1 17.4 %all-to-all-start.1 = ((f32[32,1,1152]{2,1,0:T(1,128)}), f32[32,1,1152]{2,1,0:T(1,128)S(1)}, u32[]{:S(2)}, u32[]{:S(2)}) async-start(f32[32,1,1152]{2,1,0:T(1,128)} %bitcast.9), calls=%async_computation.1 | async-start | bytes 294912 | tf_op jit(solution)/shard_map/all_to_all | solution.py:290
  47.5 3.4 %shard_map.85 = (f32[1024,128]{1,0:T(8,128)S(1)}, f32[1024,128]{1,0:T(8,128)S(1)}, f32[8,128]{1,0:T(8,128)S(1)}) custom-call(f32[256,128]{1,0:T(8,128)S(1)} %bitcast.17, f32[320,128]{1,0:T(8,128)S(1)} %collective-permute-done.inner, f32[320,128]{1,0:T(8,128)S(1)} %collective-permute-done.1.outer, f32[160,128]{1,0:T(8,128)S(1)} %collective-permute-done.2.side, ...), custom_call_target="tpu_custom_call" | custom-call | tf_op jit(solution)/shard_map/pallas_call | solution.py:239
  51.0 6.8 %all-to-all-done.1 = f32[32,1,1152]{2,1,0:T(1,128)S(1)} async-done(((f32[32,1,1152]{2,1,0:T(1,128)}), f32[32,1,1152]{2,1,0:T(1,128)S(1)}, u32[]{:S(2)}, u32[]{:S(2)}) %all-to-all-start.1) | async-done | bytes 147488 | tf_op jit(solution)/shard_map/all_to_all | solution.py:290
  57.8 2.5 %shard_map.86 = f32[64,128]{1,0:T(8,128)} custom-call(f32[288,128]{1,0:T(8,128)S(1)} %bitcast.21, f32[64,128]{1,0:T(8,128)S(1)} %get-tuple-element.27.local, f32[1024,128]{1,0:T(8,128)S(1)} %get-tuple-element.28.direct, f32[1024,128]{1,0:T(8,128)S(1)} %get-tuple-element.29.through, f32[8,128]{1,0:T(8,128)S(1)} %get-tuple-element.30.decays, ...), custom_call_target="tpu_custom_call" | custom-call | tf_op jit(solution)/shard_map/pallas_call | solution.py:239
Async XLA Ops:
  0.0 14.8 %copy-start = (f32[1,2,128,128]{3,2,1,0:T(8,128)S(1)}, f32[1,2,128,128]{3,2,1,0:T(8,128)}, u32[]{:S(2)}) copy-start(f32[1,2,128,128]{3,2,1,0:T(8,128)} %param.11) | copy-start | bytes 393220
  0.0 14.8 %copy-start.1 = (f32[32,1,2,128]{3,2,1,0:T(2,128)S(1)}, f32[32,1,2,128]{3,2,1,0:T(2,128)}, u32[]{:S(2)}) copy-start(f32[32,1,2,128]{3,2,1,0:T(2,128)} %param.9) | copy-start | bytes 98308
  0.0 14.8 %copy-start.2 = (f32[32,1,2,128]{3,2,1,0:T(2,128)S(1)}, f32[32,1,2,128]{3,2,1,0:T(2,128)}, u32[]{:S(2)}) copy-start(f32[32,1,2,128]{3,2,1,0:T(2,128)} %param.8) | copy-start | bytes 98308
  1.0 13.7 %collective-permute-start = (f32[320,128]{1,0:T(8,128)S(1)}, f32[320,128]{1,0:T(8,128)S(1)}, u32[]{:S(2)}, u32[]{:S(2)}) collective-permute-start(f32[320,128]{1,0:T(8,128)S(1)} %get-tuple-element.18), channel_id=1, source_target_pairs={{0,2},{2,0},{4,6},{6,4},{8,10},{10,8},{12,14},{14,12},{1,3},{3,1},... | collective-permute-start | bytes 491528 | tf_op jit(solution)/shard_map/ppermute | solution.py:269
  3.1 11.7 %collective-permute-start.1 = (f32[320,128]{1,0:T(8,128)S(1)}, f32[320,128]{1,0:T(8,128)S(1)}, u32[]{:S(2)}, u32[]{:S(2)}) collective-permute-start(f32[320,128]{1,0:T(8,128)S(1)} %get-tuple-element.18), channel_id=1, source_target_pairs={{2,4},{4,2},{6,8},{8,6},{10,12},{12,10},{3,5},{5,3},{7,9},{9,7},{1... | collective-permute-start | bytes 491528 | tf_op jit(solution)/shard_map/ppermute | solution.py:270
  7.2 7.5 %collective-permute-start.2 = (f32[160,128]{1,0:T(8,128)S(1)}, f32[160,128]{1,0:T(8,128)S(1)}, u32[]{:S(2)}, u32[]{:S(2)}) collective-permute-start(f32[160,128]{1,0:T(8,128)S(1)} %get-tuple-element.19), channel_id=1, source_target_pairs={{0,1},{1,0},{2,3},{3,2},{4,5},{5,4},{6,7},{7,6},{8,9},{9,8},{10,11... | collective-permute-start | bytes 245768 | tf_op jit(solution)/shard_map/ppermute | solution.py:271
  16.8 11.6 %all-to-all-start = ((f32[4,80,128]{2,1,0:T(8,128)}), f32[4,80,128]{2,1,0:T(8,128)S(1)}, u32[]{:S(2)}, u32[]{:S(2)}) async-start(f32[4,80,128]{2,1,0:T(8,128)} %bitcast.7), calls=%async_computation | async-start | bytes 327680 | tf_op jit(solution)/shard_map/all_to_all | solution.py:276
  22.7 5.7 %collective-permute-start.3 = (f32[80,128]{1,0:T(8,128)S(1)}, f32[80,128]{1,0:T(8,128)S(1)}, u32[]{:S(2)}, u32[]{:S(2)}) collective-permute-start(f32[80,128]{1,0:T(8,128)S(1)} %get-tuple-element.24.own.own2), channel_id=1, source_target_pairs={{2,4},{4,2},{6,8},{8,6},{10,12},{12,10},{3,5},{5,3},{7,9},{9,7},{1... | collective-permute-start | bytes 122888 | tf_op jit(solution)/shard_map/ppermute | solution.py:280
  30.1 27.7 %all-to-all-start.1 = ((f32[32,1,1152]{2,1,0:T(1,128)}), f32[32,1,1152]{2,1,0:T(1,128)S(1)}, u32[]{:S(2)}, u32[]{:S(2)}) async-start(f32[32,1,1152]{2,1,0:T(1,128)} %bitcast.9), calls=%async_computation.1 | async-start | bytes 294912 | tf_op jit(solution)/shard_map/all_to_all | solution.py:290

commit v3 on v2

v3 whole, which is shorter than its diff:
```python
import jax
import jax.numpy as jnp
from jax import lax
from jax.experimental import pallas as pl
from jax.experimental.pallas import tpu as pltpu
from jax.sharding import PartitionSpec as P


ALPHA = 0.05
HIGHEST = lax.Precision.HIGHEST
STEPS = 32
BLOCKS = 32
TILE = 128
PACK = 40
VECS = 9
FIRST = 22
TURNED = [(i + FIRST) % BLOCKS for i in range(BLOCKS)]
ROWS2 = 2 * PACK
f32 = jnp.float32


def mm(x, y):
    return jnp.dot(x, y, precision=HIGHEST, preferred_element_type=f32)


def mm_nt(x, y):
    return lax.dot_general(x, y, (((1,), (1,)), ((), ())), precision=HIGHEST, preferred_element_type=f32)


def mm_tn(x, y):
    return lax.dot_general(x, y, (((0,), (0,)), ((), ())), precision=HIGHEST, preferred_element_type=f32)


def rows_of(shape):
    return lax.broadcasted_iota(jnp.int32, shape, 0)


def shift_down(x, by):
    return jnp.where(rows_of(x.shape) >= by, pltpu.roll(x, by, 0), 0.0)


def recurrence(x, decay):
    for by in (1, 2, 4, 8, 16):
        x = x + decay * shift_down(x, by)
        decay = decay * decay
    return x


def power_rows(decay, first, reverse=False):
    n = rows_of((STEPS, TILE))
    exponent = (STEPS - 1 - n if reverse else n) + first
    out = jnp.ones((STEPS, TILE), f32)
    for bit in range(6):
        out = out * jnp.where((exponent >> bit) & 1 == 1, decay, 1.0)
        decay = decay * decay
    return out


def to_32(decay):
    for _ in range(5):
        decay = decay * decay
    return decay


def picked(x, index_row):
    return jnp.take_along_axis(x, jnp.broadcast_to(index_row, x.shape), axis=1, mode="promise_in_bounds")


def params(values_ref, cap_ref, p):
    total = values_ref[p : p + 1, :] + cap_ref[0, p]
    gain = 1.0 / total
    return cap_ref[0, p] * gain, gain


def coupled(p, low, high, own, side, links_ref, cond_ref, col):
    left = jnp.where(col == 1, side, 0.0) if p == 0 else own[0]
    right = own[1] if p == 0 else jnp.where(col == 0, side, 0.0)
    total = None
    for d, x in enumerate((low[p], high[p], left, right)):
        r = 2 * d + p
        term = cond_ref[r : r + 1, :] * picked(x, links_ref[r : r + 1, :])
        total = term if total is None else total + term
    return total


def every_other(ref, p, start=0):
    return ref[pl.ds(start + p, STEPS, stride=2), :]


def kernel_p(it, values, links, cond, init, copies, own, values_out, links_out, cond_out, init_out):
    own[...] = it[...]
    for k in range(4):
        copies[k * 2 * STEPS : (k + 1) * 2 * STEPS, :] = it[...]
    values_out[...] = values[...]
    links_out[...] = links[...]
    cond_out[...] = cond[...]
    init_out[...] = init[...]


def prepare(it, *small):
    vmem = pl.BlockSpec(memory_space=pltpu.VMEM)
    return pl.pallas_call(
        kernel_p,
        out_shape=[
            jax.ShapeDtypeStruct((8 * STEPS, TILE), f32),
            pltpu.VMEM(it.shape, f32),
            *[pltpu.VMEM(x.shape, x.dtype) for x in small],
        ],
        in_specs=[vmem] * (len(small) + 1),
        out_specs=[vmem] * (len(small) + 2),
    )(it, *small)


def quad_rows(start, count, height):
    odd, col = lax.axis_index("rows") % 2, lax.axis_index("cols")
    inner = ((1 - odd) * 2 + col) * 2 * height + start
    side = (odd * 2 + 1 - col) * 2 * height + jnp.where(col == 0, 0, height) + start
    return pl.ds(pl.multiple_of(inner, 8), count), pl.ds(pl.multiple_of(side, 8), count)


def kernel_a(it, src, quad, outer, bas, values, links, cond, init, cap, out, copies, near_basis):
    col = lax.axis_index("cols")
    block = lax.axis_index("tm")
    near_basis[...] = bas[pl.ds(pl.multiple_of((1 - col) * TILE, TILE), TILE), :]
    pair = lambda ref: [every_other(ref, p) for p in range(2)]
    chunk = lambda k: [every_other(quad, p, pl.multiple_of(k * 2 * STEPS, 2 * STEPS)) for p in range(2)]
    odd = lax.axis_index("rows") % 2
    inner, across, own = chunk((1 - odd) * 2 + col), chunk(odd * 2 + 1 - col), pair(it)
    sides = jnp.where(col == 0, across[0], across[1])
    lows, highs = zip(*(ordered(a, b) for a, b in zip(inner, pair(outer))))
    for p in range(2):
        basis = bas[p * TILE : (p + 1) * TILE, :]
        decay, gain = params(values, cap, p)
        force = every_other(src, p) + coupled(p, lows, highs, own, sides, links, cond, col)
        last = init[p : p + 1, :] - ALPHA * own[p][STEPS - 1 : STEPS, :]
        stacked = jnp.concatenate([force, jnp.broadcast_to(last, (8, TILE))], axis=0)
        modes = mm(stacked, basis)
        wrap = modes[STEPS : STEPS + 1, :]
        state = recurrence(modes[:STEPS] * gain, decay)
        end = state[STEPS - 1 : STEPS, :]
        end = jnp.where(block == BLOCKS - 1, ALPHA * end + wrap, end)
        row = rows_of((8, TILE))
        tail = jnp.where(row == 0, end, jnp.where(row == 1, decay, jnp.where(row == 2, wrap, 0.0)))
        first = mm_nt(state, basis)
        for ref, rows in ((out, ROWS2), (copies, 4 * ROWS2)):
            for at in range(p * PACK, rows, ROWS2):
                ref[at : at + STEPS, :] = first
                ref[at + STEPS : at + PACK, :] = tail


def kernel_b(src, own, quad, outer, bas, values, links, cond, cap, local, send):
    col = lax.axis_index("cols")
    block = lax.axis_index("tm")
    both = lambda ref, start, count: [ref[p * PACK + start : p * PACK + start + count, :] for p in range(2)]
    inner = lambda start, count: [quad[quad_rows(p * PACK + start, count, PACK)[0], :] for p in range(2)]
    side = lambda start, count: quad[quad_rows(start, count, PACK)[1], :]
    owns, sides = both(own, 0, STEPS), side(0, STEPS)
    lows, highs = zip(*(ordered(a, b) for a, b in zip(inner(0, STEPS), both(outer, 0, STEPS))))
    ends = (*both(own, STEPS, 8), *both(outer, STEPS, 8), *inner(STEPS, 8), side(STEPS, 8))
    vectors = [x[0:1, :] for x in ends]
    for p in range(2):
        basis = bas[p * TILE : (p + 1) * TILE, :]
        decay, gain = params(values, cap, p)
        force = every_other(src, p) + coupled(p, lows, highs, owns, sides, links, cond, col)
        state = recurrence(mm(force, basis) * gain, decay)
        local[p * STEPS : (p + 1) * STEPS, :] = state
        end = state[STEPS - 1 : STEPS, :]
        wrap = own[p * PACK + STEPS + 2 : p * PACK + STEPS + 3, :]
        vectors.append(jnp.where(block == BLOCKS - 1, ALPHA * end + wrap, end))
    for k, vector in enumerate(vectors):
        send[pl.ds(k, BLOCKS, stride=VECS), :] = jnp.broadcast_to(vector, (BLOCKS, TILE))


def matrices(p, neighbour, table, tie_rows, mask, bas, values, cap):
    basis = bas[p * TILE : (p + 1) * TILE, :]
    decay, gain = params(values, cap, p)
    link, weight = tie_rows
    weight = weight if mask is None else weight * mask
    direct = mm(weight * picked(neighbour.T, link), basis)
    return direct, direct * mm_tn(table, power_rows(decay, 0, reverse=True) * gain)


def ties_of(links, cond, low, high, odd):
    pick = lambda ref: jnp.where(odd, ref[high : high + 1, :], ref[low : low + 1, :])
    return pick(links), pick(cond)


def kernel_m(bas, outer, own2, quad, outer2, values, links, cond, cap, direct, through, tables, decays):
    odd = lax.axis_index("rows") % 2 == 1
    at = lambda x: x[1:2, :]
    both = lambda ref: [ref[p * PACK + STEPS : (p + 1) * PACK, :] for p in range(2)]
    inner = [quad[quad_rows(p * PACK + STEPS, 8, PACK)[0], :] for p in range(2)]
    side = quad[quad_rows(STEPS, 8, PACK)[1], :]
    for k, x in enumerate((*both(own2), *both(outer2), *inner, side)):
        decay = at(x)
        block_decay = to_32(decay)
        scale = 1.0 / (1.0 - ALPHA * to_32(block_decay))
        decays[k : k + 1, :] = block_decay
        tables[k * STEPS : (k + 1) * STEPS, :] = power_rows(decay, 1)
        tables[(7 + k) * STEPS : (8 + k) * STEPS, :] = power_rows(block_decay, 0) * scale
    decays[7:8, :] = jnp.zeros((1, TILE), f32)
    table = lambda k: tables[k * STEPS : (k + 1) * STEPS, :]
    for p in range(2):
        tile = lambda ref, q: ref[q * TILE : (q + 1) * TILE, :]
        near = 2 * (3 - p) + p
        for j, (neighbour, k, ties) in enumerate((
            (tile(outer, p), 2 + p, ties_of(links, cond, p, 2 + p, odd)),
            (tile(bas, 1 - p), 1 - p, ties_of(links, cond, near, near, odd)),
        )):
            rows = slice((2 * p + j) * TILE, (2 * p + j + 1) * TILE)
            direct[rows, :], through[rows, :] = matrices(p, neighbour, table(k), ties, None, bas, values, cap)


def kernel_n(bas, inner, side, tables, values, links, cond, cap, direct, through):
    odd = lax.axis_index("rows") % 2 == 1
    col = lax.axis_index("cols")
    table = lambda k: tables[k * STEPS : (k + 1) * STEPS, :]
    for p in range(2):
        far = 2 * (2 + p) + p
        outside = jnp.where(col == 1 - p, 1.0, 0.0)
        for j, (neighbour, k, ties, mask) in enumerate((
            (inner[p * TILE : (p + 1) * TILE, :], 4 + p, ties_of(links, cond, 2 + p, p, odd), None),
            (side[...], 6, ties_of(links, cond, far, far, odd), outside),
        )):
            rows = slice((2 * p + j) * TILE, (2 * p + j + 1) * TILE)
            direct[rows, :], through[rows, :] = matrices(p, neighbour, table(k), ties, mask, bas, values, cap)


def incoming(ends, block_decay, scaled_powers):
    summed = recurrence(ends, block_decay)
    start = ALPHA * block_decay * summed[BLOCKS - 2 : BLOCKS - 1, :] + ends[BLOCKS - 1 : BLOCKS, :]
    return shift_down(summed, 1) + scaled_powers * start


def row_at(x, index):
    return jnp.sum(jnp.where(rows_of(x.shape) == index, x, 0.0), axis=0, keepdims=True)


def kernel_c(received, local, direct1, through1, direct2, through2, tables, decays, bas, values, cap, out):
    block = lax.axis_index("tm")
    vector = lambda k: pltpu.roll(received[pl.ds(k, BLOCKS, stride=VECS), :], FIRST, 0)
    table = lambda k: tables[k * STEPS : (k + 1) * STEPS, :]
    states = [incoming(vector(k), decays[k : k + 1, :], table(7 + k)) for k in range(7)]
    paths = [table(k) * row_at(states[k], block) for k in range(7)]
    factor = jnp.where(rows_of((BLOCKS, TILE)) == BLOCKS - 1, ALPHA, 1.0)
    for p in range(2):
        basis = bas[p * TILE : (p + 1) * TILE, :]
        decay, gain = params(values, cap, p)
        span = slice(2 * p * TILE, 2 * (p + 1) * TILE)
        beside = lambda x, j, k: jnp.concatenate([x[j], x[k]], axis=1)
        product = lambda x, first, second: mm(beside(x, 2 + p, 1 - p), first[span, :]) + mm(
            beside(x, 4 + p, 6), second[span, :]
        )
        ends = vector(7 + p) + factor * product(states, through1, through2)
        entering = row_at(incoming(ends, decays[p : p + 1, :], table(7 + p)), block)
        force = product(paths, direct1, direct2)
        state = local[p * STEPS : (p + 1) * STEPS, :] + recurrence(force * gain, decay)
        state = state + table(p) * entering
        out[pl.ds(p, STEPS, stride=2), :] = mm_nt(state, basis)


def call(kernel, outs, *args, last=False):
    vmem = pl.BlockSpec(memory_space=pltpu.VMEM)
    smem = pl.BlockSpec(memory_space=pltpu.SMEM)
    shapes = [jax.ShapeDtypeStruct(out, f32) if last else pltpu.VMEM(out, f32) for out in outs]
    single = len(outs) == 1
    scalar = lambda arg: arg.shape == (1, 2)
    near = lambda arg: arg if scalar(arg) else pltpu.with_memory_space_constraint(arg, pltpu.VMEM)
    return pl.pallas_call(
        kernel,
        out_shape=shapes[0] if single else shapes,
        in_specs=[smem if scalar(arg) else vmem for arg in args],
        out_specs=vmem if single else [vmem] * len(outs),
    )(*[near(arg) for arg in args])


def swaps(first):
    return [pair for i in range(first, lax.axis_size("rows") - 1, 2) for pair in ((i, i + 1), (i + 1, i))]


def ordered(inner, outer):
    odd = lax.axis_index("rows") % 2 == 1
    return jnp.where(odd, inner, outer), jnp.where(odd, outer, inner)


def on_device(iterate, source, initial, tile_basis, tile_values, capacity, tile_links, conductance):
    it = iterate.reshape(2 * STEPS, TILE)
    src = source.reshape(2 * STEPS, TILE)
    init = initial.reshape(2, TILE)
    bas = tile_basis.reshape(2 * TILE, TILE)
    values = tile_values.reshape(2, TILE)
    links = tile_links.reshape(8, TILE)
    cond = conductance.reshape(8, TILE)
    copies, own, values, links, cond, init = prepare(it, values, links, cond, init)
    fours = [[4 * k + j for j in range(4)] for k in range(lax.axis_size("rows") // 2)]

    def exchange(own, copies):
        quad = lax.all_to_all(
            copies.reshape(4, *own.shape), ("rows", "cols"), split_axis=0, concat_axis=0, tiled=True,
            axis_index_groups=fours,
        )
        return quad.reshape(copies.shape), lax.ppermute(own, "rows", swaps(1))

    quad1, outer1 = exchange(own, copies)
    outer_basis = lax.ppermute(bas, "rows", swaps(1))
    own2, copies2, near_basis = call(
        kernel_a,
        [(ROWS2, TILE), (4 * ROWS2, TILE), (TILE, TILE)],
        own, src, quad1, outer1, bas, values, links, cond, init, capacity,
    )
    quad, outer2 = exchange(own2, copies2)
    rows_basis, _ = lax.optimization_barrier((bas, own2))
    inner_basis = lax.ppermute(rows_basis, "rows", swaps(0))
    local, send = call(
        kernel_b,
        [(2 * STEPS, TILE), (BLOCKS * VECS, TILE)],
        src, own2, quad, outer2, bas, values, links, cond, capacity,
    )
    flat = send.reshape(BLOCKS, VECS * TILE)
    received = lax.all_to_all(
        flat, "tm", split_axis=0, concat_axis=0, tiled=True, axis_index_groups=[TURNED]
    ).reshape(BLOCKS * VECS, TILE)
    near_basis, _ = lax.optimization_barrier((near_basis, send))
    side_basis = lax.ppermute(near_basis, "cols", [(0, 1), (1, 0)])
    pair_shape, table_shape = (4 * TILE, TILE), (14 * STEPS, TILE)
    direct1, through1, tables, decays = call(
        kernel_m,
        [pair_shape, pair_shape, table_shape, (8, TILE)],
        bas, outer_basis, own2, quad, outer2, values, links, cond, capacity,
    )
    direct2, through2 = call(
        kernel_n, [pair_shape, pair_shape], bas, inner_basis, side_basis, tables, values, links, cond, capacity
    )
    out = call(kernel_c, [(2 * STEPS, TILE)], received, local, direct1, through1, direct2, through2, tables, decays, bas, values, capacity, last=True)
    return out.reshape(iterate.shape)


def solution(mesh):
    in_specs = (
        P("tm", "rows", "cols", None),
        P("tm", "rows", "cols", None),
        P("rows", "cols", None),
        P("rows", "cols", None, None),
        P("rows", "cols", None),
        P("rows", "cols"),
        P(None, "rows", "cols", None),
        P(None, "rows", "cols", None),
    )
    out_specs = P("tm", "rows", "cols", None)
    return jax.shard_map(on_device, mesh=mesh, in_specs=in_specs, out_specs=out_specs, check_vma=False)
```

time: 60.7 us -> 64.2 us (1.058)
  the two profiles are of different devices: /device:TPU:11 before, /device:TPU:4 now
where the time goes in v3:
time: 64.2 us; the launch traced here: 63.6 us
  starting transfers between devices  46.3 us (72%)
  Pallas kernels  10.7 us (17%)
  waiting for transfers between devices  6.5 us (10%)
    all_to_all x1, starting transfers between devices, on_device(): lax.all_to_all(flat, 'tm', split_axis=0, concat_axis=0, tiled=True, axis_...  14.8 us
    ppermute x2, starting transfers between devices, exchange(): return (quad.reshape(copies.shape), lax.ppermute(own, 'rows', swaps(1)))  10.2 us
    all_to_all x2, starting transfers between devices, exchange(): lax.all_to_all(copies.reshape(4, *own.shape), ('rows', 'cols'), split_axi...  9.39 us
    pallas_call x5, Pallas kernels, call(): pl.pallas_call(kernel, out_shape=shapes[0] if single else shapes, in_spec...  9.23 us
    ppermute x1, starting transfers between devices, on_device(): side_basis = lax.ppermute(near_basis, 'cols', [(0, 1), (1, 0)])  5.44 us
    ppermute x2, waiting for transfers between devices, exchange(): return (quad.reshape(copies.shape), lax.ppermute(own, 'rows', swaps(1)))  4.76 us
    ppermute x1, starting transfers between devices, on_device(): outer_basis = lax.ppermute(bas, 'rows', swaps(1))  3.9 us
    ppermute x1, starting transfers between devices, on_device(): inner_basis = lax.ppermute(rows_basis, 'rows', swaps(0))  2.57 us
  transfers between devices with their start and end apart: 8, of which 3 were waited for; matrix products, arithmetic and copies ran while one was open for 0% of the time, Pallas kernels for 5%

profile of v3, /device:TPU:4, one launch (start us, length us, event | category | flops | bytes accessed | tf_op | source)
XLA Modules:
  0.0 63.6 jit_solution(14324013187937948977)
XLA Ops:
  0.0 1.5 %shard_map.82 = (f32[256,128]{1,0:T(8,128)}, f32[64,128]{1,0:T(8,128)S(1)}, f32[2,128]{1,0:T(2,128)S(1)}, s32[8,128]{1,0:T(8,128)S(1)}, f32[8,128]{1,0:T(8,128)S(1)}, /*index=5*/f32[2,128]{1,0:T(2,128)S(1)}) custom-call(f32[64,128]{1,0:T(8,128)} %bitcast.30, f32[2,128]{1,0:T(2,128)} %bitcast.33, s32[8,128]{1,0:T(8,128)} %bitcast.31, f32[8,128]{1,0:T(8,128)} %bitcast.32, ...), custom_call_target="tpu_custom_call" | custom-call | tf_op jit(solution)/shard_map/pallas_call | solution.py:102
  1.5 0.0 copy-start
  1.5 0.0 copy-start.1
  1.5 4.6 %all-to-all-start = ((f32[4,64,128]{2,1,0:T(8,128)}), f32[4,64,128]{2,1,0:T(8,128)S(1)}, u32[]{:S(2)}, u32[]{:S(2)}) async-start(f32[4,64,128]{2,1,0:T(8,128)} %bitcast.29), calls=%async_computation | async-start | bytes 262144 | tf_op jit(solution)/shard_map/all_to_all | solution.py:298
  6.1 3.9 %collective-permute-start = (f32[64,128]{1,0:T(8,128)S(1)}, f32[64,128]{1,0:T(8,128)S(1)}, u32[]{:S(2)}, u32[]{:S(2)}) collective-permute-start(f32[64,128]{1,0:T(8,128)S(1)} %get-tuple-element.24.it), channel_id=1, source_target_pairs={{2,4},{4,2},{6,8},{8,6},{10,12},{12,10},{3,5},{5,3},{7,9},{9,7},{1... | collective-permute-start | bytes 98312 | tf_op jit(solution)/shard_map/ppermute | solution.py:302
  10.0 2.8 %collective-permute-done.outer = f32[64,128]{1,0:T(8,128)S(1)} collective-permute-done((f32[64,128]{1,0:T(8,128)S(1)}, f32[64,128]{1,0:T(8,128)S(1)}, u32[]{:S(2)}, u32[]{:S(2)}) %collective-permute-start) | collective-permute-done | bytes 32800 | tf_op jit(solution)/shard_map/ppermute | solution.py:302
  12.8 0.0 all-to-all-done
  12.8 0.0 copy-done
  12.8 0.0 copy-done.1
  12.8 2.1 %shard_map.83 = (f32[80,128]{1,0:T(8,128)S(1)}, f32[320,128]{1,0:T(8,128)}, f32[128,128]{1,0:T(8,128)S(1)}) custom-call(f32[64,128]{1,0:T(8,128)S(1)} %get-tuple-element.24.it, f32[64,128]{1,0:T(8,128)S(1)} %bitcast.27, f32[256,128]{1,0:T(8,128)S(1)} %bitcast.26, f32[64,128]{1,0:T(8,128)S(1)} %collective-permute-done.outer, f32[256,128]{1,0:T(8,128)S(1)} %bitcast.16, ...), custom_call_target="tpu_custom_call" | custom-call | tf_op jit(solution)/shard_map/pallas_call | solution.py:269
  14.8 4.8 %all-to-all-start.1 = ((f32[4,80,128]{2,1,0:T(8,128)}), f32[4,80,128]{2,1,0:T(8,128)S(1)}, u32[]{:S(2)}, u32[]{:S(2)}) async-start(f32[4,80,128]{2,1,0:T(8,128)} %bitcast.9), calls=%async_computation.1 | async-start | bytes 327680 | tf_op jit(solution)/shard_map/all_to_all | solution.py:298
  19.6 6.3 %collective-permute-start.1 = (f32[80,128]{1,0:T(8,128)S(1)}, f32[80,128]{1,0:T(8,128)S(1)}, u32[]{:S(2)}, u32[]{:S(2)}) collective-permute-start(f32[80,128]{1,0:T(8,128)S(1)} %get-tuple-element.30.own.own2), channel_id=1, source_target_pairs={{2,4},{4,2},{6,8},{8,6},{10,12},{12,10},{3,5},{5,3},{7,9},{9,7},{1... | collective-permute-start | bytes 122888 | tf_op jit(solution)/shard_map/ppermute | solution.py:302
  25.9 2.0 %collective-permute-done.1.outer.outer2 = f32[80,128]{1,0:T(8,128)S(1)} collective-permute-done((f32[80,128]{1,0:T(8,128)S(1)}, f32[80,128]{1,0:T(8,128)S(1)}, u32[]{:S(2)}, u32[]{:S(2)}) %collective-permute-start.1) | collective-permute-done | bytes 40992 | tf_op jit(solution)/shard_map/ppermute | solution.py:302
  27.9 0.0 all-to-all-done.1
  27.9 1.7 %shard_map.84 = (f32[64,128]{1,0:T(8,128)S(1)}, f32[288,128]{1,0:T(8,128)}) custom-call(f32[64,128]{1,0:T(8,128)S(1)} %bitcast.28, f32[80,128]{1,0:T(8,128)S(1)} %get-tuple-element.30.own.own2, f32[320,128]{1,0:T(8,128)S(1)} %bitcast.23, f32[80,128]{1,0:T(8,128)S(1)} %collective-permute-done.1.outer.outer2, f32[256,128]{1,0:T(8,128)S(1)} %bitcast.17, ...), custom_call_target="tpu_custom_call" | custom-call | tf_op jit(solution)/shard_map/pallas_call | solution.py:269
  29.6 14.8 %all-to-all-start.2 = ((f32[32,1,1152]{2,1,0:T(1,128)}), f32[32,1,1152]{2,1,0:T(1,128)S(1)}, u32[]{:S(2)}, u32[]{:S(2)}) async-start(f32[32,1,1152]{2,1,0:T(1,128)} %bitcast.11), calls=%async_computation.2 | async-start | bytes 294912 | tf_op jit(solution)/shard_map/all_to_all | solution.py:320
  44.4 3.9 %collective-permute-start.2 = (f32[256,128]{1,0:T(8,128)S(1)}, f32[256,128]{1,0:T(8,128)S(1)}, u32[]{:S(2)}, u32[]{:S(2)}) collective-permute-start(f32[256,128]{1,0:T(8,128)S(1)} %bitcast.18), channel_id=1, source_target_pairs={{2,4},{4,2},{6,8},{8,6},{10,12},{12,10},{3,5},{5,3},{7,9},{9,7},{1... | collective-permute-start | bytes 393224 | tf_op jit(solution)/shard_map/ppermute | solution.py:305
  48.3 2.6 %collective-permute-start.3 = (f32[256,128]{1,0:T(8,128)S(1)}, f32[256,128]{1,0:T(8,128)S(1)}, u32[]{:S(2)}, u32[]{:S(2)}) collective-permute-start(f32[256,128]{1,0:T(8,128)S(1)} %bitcast.19), channel_id=1, source_target_pairs={{0,2},{2,0},{4,6},{6,4},{8,10},{10,8},{12,14},{14,12},{1,3},{3,1},... | collective-permute-start | bytes 393224 | tf_op jit(solution)/shard_map/ppermute | solution.py:313
  50.9 5.4 %collective-permute-start.4 = (f32[128,128]{1,0:T(8,128)S(1)}, f32[128,128]{1,0:T(8,128)S(1)}, u32[]{:S(2)}, u32[]{:S(2)}) collective-permute-start(f32[128,128]{1,0:T(8,128)S(1)} %get-tuple-element.38), channel_id=1, source_target_pairs={{0,1},{1,0},{2,3},{3,2},{4,5},{5,4},{6,7},{7,6},{8,9},{9,8},{10,11... | collective-permute-start | bytes 196616 | tf_op jit(solution)/shard_map/ppermute | solution.py:324
  56.4 0.0 collective-permute-done.2.outer
  56.4 1.5 %shard_map.85 = (f32[512,128]{1,0:T(8,128)S(1)}, f32[512,128]{1,0:T(8,128)S(1)}, f32[448,128]{1,0:T(8,128)S(1)}, f32[8,128]{1,0:T(8,128)S(1)}) custom-call(f32[256,128]{1,0:T(8,128)S(1)} %bitcast.20, f32[256,128]{1,0:T(8,128)S(1)} %collective-permute-done.2.outer, f32[80,128]{1,0:T(8,128)S(1)} %get-tuple-element.30.own.own2, f32[320,128]{1,0:T(8,128)S(1)} %bitcast.24, ...), custom_call_target="tpu_custom_call" | custom-call | tf_op jit(solution)/shard_map/pallas_call | solution.py:269
  57.9 0.0 collective-permute-done.3.inner
  57.9 1.7 %collective-permute-done.4.side = f32[128,128]{1,0:T(8,128)S(1)} collective-permute-done((f32[128,128]{1,0:T(8,128)S(1)}, f32[128,128]{1,0:T(8,128)S(1)}, u32[]{:S(2)}, u32[]{:S(2)}) %collective-permute-start.4) | collective-permute-done | bytes 65568 | tf_op jit(solution)/shard_map/ppermute | solution.py:324
  59.6 1.5 %shard_map.86 = (f32[512,128]{1,0:T(8,128)S(1)}, f32[512,128]{1,0:T(8,128)S(1)}) custom-call(f32[256,128]{1,0:T(8,128)S(1)} %bitcast.21, f32[256,128]{1,0:T(8,128)S(1)} %collective-permute-done.3.inner, f32[128,128]{1,0:T(8,128)S(1)} %collective-permute-done.4.side, f32[448,128]{1,0:T(8,128)S(1)} %get-tuple-element.39.tables, ...), custom_call_target="tpu_custom_call" | custom-call | tf_op jit(solution)/shard_map/pallas_call | solution.py:269
  61.1 0.0 all-to-all-done.2
  61.1 2.5 %shard_map.87 = f32[64,128]{1,0:T(8,128)} custom-call(f32[288,128]{1,0:T(8,128)S(1)} %bitcast.25, f32[64,128]{1,0:T(8,128)S(1)} %get-tuple-element.33.local, f32[512,128]{1,0:T(8,128)S(1)} %get-tuple-element.34.direct1, f32[512,128]{1,0:T(8,128)S(1)} %get-tuple-element.35.through1, f32[512,128]{1,0:T(8,128)S(1)} %get-tuple-element.40.direct2, ...), custom_call_target="tpu_custom_call" | custom-call | tf_op jit(solution)/shard_map/pallas_call | solution.py:269
Async XLA Ops:
  1.5 11.3 %copy-start = (f32[1,2,128,128]{3,2,1,0:T(8,128)S(1)}, f32[1,2,128,128]{3,2,1,0:T(8,128)}, u32[]{:S(2)}) copy-start(f32[1,2,128,128]{3,2,1,0:T(8,128)} %param.11) | copy-start | bytes 393220
  1.5 11.3 %copy-start.1 = (f32[32,1,2,128]{3,2,1,0:T(2,128)S(1)}, f32[32,1,2,128]{3,2,1,0:T(2,128)}, u32[]{:S(2)}) copy-start(f32[32,1,2,128]{3,2,1,0:T(2,128)} %param.9) | copy-start | bytes 98308
  1.5 11.3 %all-to-all-start = ((f32[4,64,128]{2,1,0:T(8,128)}), f32[4,64,128]{2,1,0:T(8,128)S(1)}, u32[]{:S(2)}, u32[]{:S(2)}) async-start(f32[4,64,128]{2,1,0:T(8,128)} %bitcast.29), calls=%async_computation | async-start | bytes 262144 | tf_op jit(solution)/shard_map/all_to_all | solution.py:298
  6.1 6.7 %collective-permute-start = (f32[64,128]{1,0:T(8,128)S(1)}, f32[64,128]{1,0:T(8,128)S(1)}, u32[]{:S(2)}, u32[]{:S(2)}) collective-permute-start(f32[64,128]{1,0:T(8,128)S(1)} %get-tuple-element.24.it), channel_id=1, source_target_pairs={{2,4},{4,2},{6,8},{8,6},{10,12},{12,10},{3,5},{5,3},{7,9},{9,7},{1... | collective-permute-start | bytes 98312 | tf_op jit(solution)/shard_map/ppermute | solution.py:302
  14.8 13.1 %all-to-all-start.1 = ((f32[4,80,128]{2,1,0:T(8,128)}), f32[4,80,128]{2,1,0:T(8,128)S(1)}, u32[]{:S(2)}, u32[]{:S(2)}) async-start(f32[4,80,128]{2,1,0:T(8,128)} %bitcast.9), calls=%async_computation.1 | async-start | bytes 327680 | tf_op jit(solution)/shard_map/all_to_all | solution.py:298
  19.6 8.3 %collective-permute-start.1 = (f32[80,128]{1,0:T(8,128)S(1)}, f32[80,128]{1,0:T(8,128)S(1)}, u32[]{:S(2)}, u32[]{:S(2)}) collective-permute-start(f32[80,128]{1,0:T(8,128)S(1)} %get-tuple-element.30.own.own2), channel_id=1, source_target_pairs={{2,4},{4,2},{6,8},{8,6},{10,12},{12,10},{3,5},{5,3},{7,9},{9,7},{1... | collective-permute-start | bytes 122888 | tf_op jit(solution)/shard_map/ppermute | solution.py:302
  29.6 31.5 %all-to-all-start.2 = ((f32[32,1,1152]{2,1,0:T(1,128)}), f32[32,1,1152]{2,1,0:T(1,128)S(1)}, u32[]{:S(2)}, u32[]{:S(2)}) async-start(f32[32,1,1152]{2,1,0:T(1,128)} %bitcast.11), calls=%async_computation.2 | async-start | bytes 294912 | tf_op jit(solution)/shard_map/all_to_all | solution.py:320
  44.4 11.9 %collective-permute-start.2 = (f32[256,128]{1,0:T(8,128)S(1)}, f32[256,128]{1,0:T(8,128)S(1)}, u32[]{:S(2)}, u32[]{:S(2)}) collective-permute-start(f32[256,128]{1,0:T(8,128)S(1)} %bitcast.18), channel_id=1, source_target_pairs={{2,4},{4,2},{6,8},{8,6},{10,12},{12,10},{3,5},{5,3},{7,9},{9,7},{1... | collective-permute-start | bytes 393224 | tf_op jit(solution)/shard_map/ppermute | solution.py:305
  48.3 9.6 %collective-permute-start.3 = (f32[256,128]{1,0:T(8,128)S(1)}, f32[256,128]{1,0:T(8,128)S(1)}, u32[]{:S(2)}, u32[]{:S(2)}) collective-permute-start(f32[256,128]{1,0:T(8,128)S(1)} %bitcast.19), channel_id=1, source_target_pairs={{0,2},{2,0},{4,6},{6,4},{8,10},{10,8},{12,14},{14,12},{1,3},{3,1},... | collective-permute-start | bytes 393224 | tf_op jit(solution)/shard_map/ppermute | solution.py:313
  50.9 8.7 %collective-permute-start.4 = (f32[128,128]{1,0:T(8,128)S(1)}, f32[128,128]{1,0:T(8,128)S(1)}, u32[]{:S(2)}, u32[]{:S(2)}) collective-permute-start(f32[128,128]{1,0:T(8,128)S(1)} %get-tuple-element.38), channel_id=1, source_target_pairs={{0,1},{1,0},{2,3},{3,2},{4,5},{5,4},{6,7},{7,6},{8,9},{9,8},{10,11... | collective-permute-start | bytes 196616 | tf_op jit(solution)/shard_map/ppermute | solution.py:324

commit v4 on v3

--- a/solution.py
+++ b/solution.py
@@ -13,7 +13,7 @@
 TILE = 128
 PACK = 40
 VECS = 9
-FIRST = 22
+FIRST = 20
 TURNED = [(i + FIRST) % BLOCKS for i in range(BLOCKS)]
 ROWS2 = 2 * PACK
 f32 = jnp.float32
@@ -66,10 +66,8 @@
     return jnp.take_along_axis(x, jnp.broadcast_to(index_row, x.shape), axis=1, mode="promise_in_bounds")
 
 
-def params(values_ref, cap_ref, p):
-    total = values_ref[p : p + 1, :] + cap_ref[0, p]
-    gain = 1.0 / total
-    return cap_ref[0, p] * gain, gain
+def params(coef, p):
+    return coef[p : p + 1, :], coef[2 + p : 3 + p, :]
 
 
 def coupled(p, low, high, own, side, links_ref, cond_ref, col):
@@ -87,28 +85,33 @@
     return ref[pl.ds(start + p, STEPS, stride=2), :]
 
 
-def kernel_p(it, values, links, cond, init, copies, own, values_out, links_out, cond_out, init_out):
+def kernel_p(it, links, cond, init, values, cap, copies, own, links_out, cond_out, init_out, coef):
     own[...] = it[...]
     for k in range(4):
         copies[k * 2 * STEPS : (k + 1) * 2 * STEPS, :] = it[...]
-    values_out[...] = values[...]
+    for p in range(2):
+        capacity = jnp.broadcast_to(cap[0:1, p : p + 1], (1, TILE))
+        gain = 1.0 / (values[p : p + 1, :] + capacity)
+        coef[p : p + 1, :] = capacity * gain
+        coef[2 + p : 3 + p, :] = gain
     links_out[...] = links[...]
     cond_out[...] = cond[...]
     init_out[...] = init[...]
 
 
-def prepare(it, *small):
+def prepare(it, *rest):
     vmem = pl.BlockSpec(memory_space=pltpu.VMEM)
     return pl.pallas_call(
         kernel_p,
         out_shape=[
             jax.ShapeDtypeStruct((8 * STEPS, TILE), f32),
             pltpu.VMEM(it.shape, f32),
-            *[pltpu.VMEM(x.shape, x.dtype) for x in small],
+            *[pltpu.VMEM(x.shape, x.dtype) for x in rest[:3]],
+            pltpu.VMEM((4, TILE), f32),
         ],
-        in_specs=[vmem] * (len(small) + 1),
-        out_specs=[vmem] * (len(small) + 2),
-    )(it, *small)
+        in_specs=[vmem] * 6,
+        out_specs=[vmem] * 6,
+    )(it, *rest)
 
 
 def quad_rows(start, count, height):
@@ -118,7 +121,7 @@
     return pl.ds(pl.multiple_of(inner, 8), count), pl.ds(pl.multiple_of(side, 8), count)
 
 
-def kernel_a(it, src, quad, outer, bas, values, links, cond, init, cap, out, copies, near_basis):
+def kernel_a(it, src, quad, outer, bas, links, cond, init, coef, out, copies, near_basis):
     col = lax.axis_index("cols")
     block = lax.axis_index("tm")
     near_basis[...] = bas[pl.ds(pl.multiple_of((1 - col) * TILE, TILE), TILE), :]
@@ -130,7 +133,7 @@
     lows, highs = zip(*(ordered(a, b) for a, b in zip(inner, pair(outer))))
     for p in range(2):
         basis = bas[p * TILE : (p + 1) * TILE, :]
-        decay, gain = params(values, cap, p)
+        decay, gain = params(coef, p)
         force = every_other(src, p) + coupled(p, lows, highs, own, sides, links, cond, col)
         last = init[p : p + 1, :] - ALPHA * own[p][STEPS - 1 : STEPS, :]
         stacked = jnp.concatenate([force, jnp.broadcast_to(last, (8, TILE))], axis=0)
@@ -148,7 +151,7 @@
                 ref[at + STEPS : at + PACK, :] = tail
 
 
-def kernel_b(src, own, quad, outer, bas, values, links, cond, cap, local, send):
+def kernel_b(src, own, quad, outer, bas, links, cond, coef, local, send):
     col = lax.axis_index("cols")
     block = lax.axis_index("tm")
     both = lambda ref, start, count: [ref[p * PACK + start : p * PACK + start + count, :] for p in range(2)]
@@ -160,7 +163,7 @@
     vectors = [x[0:1, :] for x in ends]
     for p in range(2):
         basis = bas[p * TILE : (p + 1) * TILE, :]
-        decay, gain = params(values, cap, p)
+        decay, gain = params(coef, p)
         force = every_other(src, p) + coupled(p, lows, highs, owns, sides, links, cond, col)
         state = recurrence(mm(force, basis) * gain, decay)
         local[p * STEPS : (p + 1) * STEPS, :] = state
@@ -171,9 +174,9 @@
         send[pl.ds(k, BLOCKS, stride=VECS), :] = jnp.broadcast_to(vector, (BLOCKS, TILE))
 
 
-def matrices(p, neighbour, table, tie_rows, mask, bas, values, cap):
+def matrices(p, neighbour, table, tie_rows, mask, bas, coef):
     basis = bas[p * TILE : (p + 1) * TILE, :]
-    decay, gain = params(values, cap, p)
+    decay, gain = params(coef, p)
     link, weight = tie_rows
     weight = weight if mask is None else weight * mask
     direct = mm(weight * picked(neighbour.T, link), basis)
@@ -185,7 +188,7 @@
     return pick(links), pick(cond)
 
 
-def kernel_m(bas, outer, own2, quad, outer2, values, links, cond, cap, direct, through, tables, decays):
+def kernel_m(bas, outer, own2, quad, outer2, links, cond, coef, direct, through, tables, decays):
     odd = lax.axis_index("rows") % 2 == 1
     at = lambda x: x[1:2, :]
     both = lambda ref: [ref[p * PACK + STEPS : (p + 1) * PACK, :] for p in range(2)]
@@ -208,10 +211,10 @@
             (tile(bas, 1 - p), 1 - p, ties_of(links, cond, near, near, odd)),
         )):
             rows = slice((2 * p + j) * TILE, (2 * p + j + 1) * TILE)
-            direct[rows, :], through[rows, :] = matrices(p, neighbour, table(k), ties, None, bas, values, cap)
-
-
-def kernel_n(bas, inner, side, tables, values, links, cond, cap, direct, through):
+            direct[rows, :], through[rows, :] = matrices(p, neighbour, table(k), ties, None, bas, coef)
+
+
+def kernel_n(bas, inner, side, tables, links, cond, coef, direct, through):
     odd = lax.axis_index("rows") % 2 == 1
     col = lax.axis_index("cols")
     table = lambda k: tables[k * STEPS : (k + 1) * STEPS, :]
@@ -223,7 +226,7 @@
             (side[...], 6, ties_of(links, cond, far, far, odd), outside),
         )):
             rows = slice((2 * p + j) * TILE, (2 * p + j + 1) * TILE)
-            direct[rows, :], through[rows, :] = matrices(p, neighbour, table(k), ties, mask, bas, values, cap)
+            direct[rows, :], through[rows, :] = matrices(p, neighbour, table(k), ties, mask, bas, coef)
 
 
 def incoming(ends, block_decay, scaled_powers):
@@ -236,7 +239,7 @@
     return jnp.sum(jnp.where(rows_of(x.shape) == index, x, 0.0), axis=0, keepdims=True)
 
 
-def kernel_c(received, local, direct1, through1, direct2, through2, tables, decays, bas, values, cap, out):
+def kernel_c(received, local, direct1, through1, direct2, through2, tables, decays, bas, coef, out):
     block = lax.axis_index("tm")
     vector = lambda k: pltpu.roll(received[pl.ds(k, BLOCKS, stride=VECS), :], FIRST, 0)
     table = lambda k: tables[k * STEPS : (k + 1) * STEPS, :]
@@ -245,7 +248,7 @@
     factor = jnp.where(rows_of((BLOCKS, TILE)) == BLOCKS - 1, ALPHA, 1.0)
     for p in range(2):
         basis = bas[p * TILE : (p + 1) * TILE, :]
-        decay, gain = params(values, cap, p)
+        decay, gain = params(coef, p)
         span = slice(2 * p * TILE, 2 * (p + 1) * TILE)
         beside = lambda x, j, k: jnp.concatenate([x[j], x[k]], axis=1)
         product = lambda x, first, second: mm(beside(x, 2 + p, 1 - p), first[span, :]) + mm(
@@ -261,17 +264,14 @@
 
 def call(kernel, outs, *args, last=False):
     vmem = pl.BlockSpec(memory_space=pltpu.VMEM)
-    smem = pl.BlockSpec(memory_space=pltpu.SMEM)
     shapes = [jax.ShapeDtypeStruct(out, f32) if last else pltpu.VMEM(out, f32) for out in outs]
     single = len(outs) == 1
-    scalar = lambda arg: arg.shape == (1, 2)
-    near = lambda arg: arg if scalar(arg) else pltpu.with_memory_space_constraint(arg, pltpu.VMEM)
     return pl.pallas_call(
         kernel,
         out_shape=shapes[0] if single else shapes,
-        in_specs=[smem if scalar(arg) else vmem for arg in args],
+        in_specs=[vmem] * len(args),
         out_specs=vmem if single else [vmem] * len(outs),
-    )(*[near(arg) for arg in args])
+    )(*[pltpu.with_memory_space_constraint(arg, pltpu.VMEM) for arg in args])
 
 
 def swaps(first):
@@ -291,7 +291,7 @@
     values = tile_values.reshape(2, TILE)
     links = tile_links.reshape(8, TILE)
     cond = conductance.reshape(8, TILE)
-    copies, own, values, links, cond, init = prepare(it, values, links, cond, init)
+    copies, own, links, cond, init, coef = prepare(it, links, cond, init, values, capacity)
     fours = [[4 * k + j for j in range(4)] for k in range(lax.axis_size("rows") // 2)]
 
     def exchange(own, copies):
@@ -306,7 +306,7 @@
     own2, copies2, near_basis = call(
         kernel_a,
         [(ROWS2, TILE), (4 * ROWS2, TILE), (TILE, TILE)],
-        own, src, quad1, outer1, bas, values, links, cond, init, capacity,
+        own, src, quad1, outer1, bas, links, cond, init, coef,
     )
     quad, outer2 = exchange(own2, copies2)
     rows_basis, _ = lax.optimization_barrier((bas, own2))
@@ -314,7 +314,7 @@
     local, send = call(
         kernel_b,
         [(2 * STEPS, TILE), (BLOCKS * VECS, TILE)],
-        src, own2, quad, outer2, bas, values, links, cond, capacity,
+        src, own2, quad, outer2, bas, links, cond, coef,
     )
     flat = send.reshape(BLOCKS, VECS * TILE)
     received = lax.all_to_all(
@@ -326,12 +326,12 @@
     direct1, through1, tables, decays = call(
         kernel_m,
         [pair_shape, pair_shape, table_shape, (8, TILE)],
-        bas, outer_basis, own2, quad, outer2, values, links, cond, capacity,
+        bas, outer_basis, own2, quad, outer2, links, cond, coef,
     )
     direct2, through2 = call(
-        kernel_n, [pair_shape, pair_shape], bas, inner_basis, side_basis, tables, values, links, cond, capacity
-    )
-    out = call(kernel_c, [(2 * STEPS, TILE)], received, local, direct1, through1, direct2, through2, tables, decays, bas, values, capacity, last=True)
+        kernel_n, [pair_shape, pair_shape], bas, inner_basis, side_basis, tables, links, cond, coef
+    )
+    out = call(kernel_c, [(2 * STEPS, TILE)], received, local, direct1, through1, direct2, through2, tables, decays, bas, coef, last=True)
     return out.reshape(iterate.shape)
 
 

time: 64.2 us -> 62.4 us (0.972)
  Pallas kernels: 10.7 us -> 7.43 us
  starting transfers between devices: 46.3 us -> 47.2 us
    pallas_call x5, Pallas kernels: 9.23 us -> 5.97 us  [call(): pl.pallas_call(kernel, out_shape=shapes[0] if single else shapes, in_spec...]
    all_to_all x1, starting transfers between devices: 14.8 us -> 15.7 us  [on_device(): lax.all_to_all(flat, 'tm', split_axis=0, concat_axis=0, tiled=True, axis_...]
  transfers between devices with their start and end apart: 8 -> 8, of which waited for: 3 -> 3; matrix products, arithmetic and copies ran while one was open for 0% -> 0% of each run, Pallas kernels for 5% -> 3%
where the time goes in v4:
time: 62.4 us; the launch traced here: 61.9 us
  starting transfers between devices  47.2 us (76%)
  Pallas kernels  7.43 us (12%)
  waiting for transfers between devices  7.13 us (11%)
    all_to_all x1, starting transfers between devices, on_device(): lax.all_to_all(flat, 'tm', split_axis=0, concat_axis=0, tiled=True, axis_...  15.7 us
    ppermute x2, starting transfers between devices, exchange(): return (quad.reshape(copies.shape), lax.ppermute(own, 'rows', swaps(1)))  10.2 us
    all_to_all x2, starting transfers between devices, exchange(): lax.all_to_all(copies.reshape(4, *own.shape), ('rows', 'cols'), split_axi...  9.39 us
    pallas_call x5, Pallas kernels, call(): pl.pallas_call(kernel, out_shape=shapes[0] if single else shapes, in_spec...  5.97 us
    ppermute x1, starting transfers between devices, on_device(): side_basis = lax.ppermute(near_basis, 'cols', [(0, 1), (1, 0)])  5.44 us
    ppermute x2, waiting for transfers between devices, exchange(): return (quad.reshape(copies.shape), lax.ppermute(own, 'rows', swaps(1)))  4.76 us
    ppermute x1, starting transfers between devices, on_device(): outer_basis = lax.ppermute(bas, 'rows', swaps(1))  3.9 us
    ppermute x1, starting transfers between devices, on_device(): inner_basis = lax.ppermute(rows_basis, 'rows', swaps(0))  2.57 us
  transfers between devices with their start and end apart: 8, of which 3 were waited for; matrix products, arithmetic and copies ran while one was open for 0% of the time, Pallas kernels for 3%

profile of v4, /device:TPU:4, one launch (start us, length us, event | category | flops | bytes accessed | tf_op | source)
XLA Modules:
  0.0 61.9 jit_solution(3393886585358297562)
XLA Ops:
  0.0 1.5 %shard_map.82 = (f32[256,128]{1,0:T(8,128)}, f32[64,128]{1,0:T(8,128)S(1)}, s32[8,128]{1,0:T(8,128)S(1)}, f32[8,128]{1,0:T(8,128)S(1)}, f32[2,128]{1,0:T(2,128)S(1)}, /*index=5*/f32[4,128]{1,0:T(4,128)S(1)}) custom-call(f32[64,128]{1,0:T(8,128)} %bitcast.30, s32[8,128]{1,0:T(8,128)} %bitcast.31, f32[8,128]{1,0:T(8,128)} %bitcast.32, f32[2,128]{1,0:T(2,128)} %bitcast.33, ...), custom_call_target="tpu_custom_call" | custom-call | tf_op jit(solution)/shard_map/pallas_call | solution.py:104
  1.5 0.0 copy-start
  1.5 0.0 copy-start.1
  1.5 4.6 %all-to-all-start = ((f32[4,64,128]{2,1,0:T(8,128)}), f32[4,64,128]{2,1,0:T(8,128)S(1)}, u32[]{:S(2)}, u32[]{:S(2)}) async-start(f32[4,64,128]{2,1,0:T(8,128)} %bitcast.29), calls=%async_computation | async-start | bytes 262144 | tf_op jit(solution)/shard_map/all_to_all | solution.py:298
  6.1 3.9 %collective-permute-start = (f32[64,128]{1,0:T(8,128)S(1)}, f32[64,128]{1,0:T(8,128)S(1)}, u32[]{:S(2)}, u32[]{:S(2)}) collective-permute-start(f32[64,128]{1,0:T(8,128)S(1)} %get-tuple-element.24.it), channel_id=1, source_target_pairs={{2,4},{4,2},{6,8},{8,6},{10,12},{12,10},{3,5},{5,3},{7,9},{9,7},{1... | collective-permute-start | bytes 98312 | tf_op jit(solution)/shard_map/ppermute | solution.py:302
  10.0 2.8 %collective-permute-done.outer = f32[64,128]{1,0:T(8,128)S(1)} collective-permute-done((f32[64,128]{1,0:T(8,128)S(1)}, f32[64,128]{1,0:T(8,128)S(1)}, u32[]{:S(2)}, u32[]{:S(2)}) %collective-permute-start) | collective-permute-done | bytes 32800 | tf_op jit(solution)/shard_map/ppermute | solution.py:302
  12.8 0.0 all-to-all-done
  12.8 0.0 copy-done
  12.8 0.0 copy-done.1
  12.8 1.4 %shard_map.83 = (f32[80,128]{1,0:T(8,128)S(1)}, f32[320,128]{1,0:T(8,128)}, f32[128,128]{1,0:T(8,128)S(1)}) custom-call(f32[64,128]{1,0:T(8,128)S(1)} %get-tuple-element.24.it, f32[64,128]{1,0:T(8,128)S(1)} %bitcast.27, f32[256,128]{1,0:T(8,128)S(1)} %bitcast.26, f32[64,128]{1,0:T(8,128)S(1)} %collective-permute-done.outer, f32[256,128]{1,0:T(8,128)S(1)} %bitcast.16, ...), custom_call_target="tpu_custom_call" | custom-call | tf_op jit(solution)/shard_map/pallas_call | solution.py:269
  14.2 4.8 %all-to-all-start.1 = ((f32[4,80,128]{2,1,0:T(8,128)}), f32[4,80,128]{2,1,0:T(8,128)S(1)}, u32[]{:S(2)}, u32[]{:S(2)}) async-start(f32[4,80,128]{2,1,0:T(8,128)} %bitcast.9), calls=%async_computation.1 | async-start | bytes 327680 | tf_op jit(solution)/shard_map/all_to_all | solution.py:298
  19.0 6.3 %collective-permute-start.1 = (f32[80,128]{1,0:T(8,128)S(1)}, f32[80,128]{1,0:T(8,128)S(1)}, u32[]{:S(2)}, u32[]{:S(2)}) collective-permute-start(f32[80,128]{1,0:T(8,128)S(1)} %get-tuple-element.30.own.own2), channel_id=1, source_target_pairs={{2,4},{4,2},{6,8},{8,6},{10,12},{12,10},{3,5},{5,3},{7,9},{9,7},{1... | collective-permute-start | bytes 122888 | tf_op jit(solution)/shard_map/ppermute | solution.py:302
  25.3 2.0 %collective-permute-done.1.outer.outer2 = f32[80,128]{1,0:T(8,128)S(1)} collective-permute-done((f32[80,128]{1,0:T(8,128)S(1)}, f32[80,128]{1,0:T(8,128)S(1)}, u32[]{:S(2)}, u32[]{:S(2)}) %collective-permute-start.1) | collective-permute-done | bytes 40992 | tf_op jit(solution)/shard_map/ppermute | solution.py:302
  27.2 0.0 all-to-all-done.1
  27.2 1.0 %shard_map.84 = (f32[64,128]{1,0:T(8,128)S(1)}, f32[288,128]{1,0:T(8,128)}) custom-call(f32[64,128]{1,0:T(8,128)S(1)} %bitcast.28, f32[80,128]{1,0:T(8,128)S(1)} %get-tuple-element.30.own.own2, f32[320,128]{1,0:T(8,128)S(1)} %bitcast.23, f32[80,128]{1,0:T(8,128)S(1)} %collective-permute-done.1.outer.outer2, f32[256,128]{1,0:T(8,128)S(1)} %bitcast.17, ...), custom_call_target="tpu_custom_call" | custom-call | tf_op jit(solution)/shard_map/pallas_call | solution.py:269
  28.3 15.7 %all-to-all-start.2 = ((f32[32,1,1152]{2,1,0:T(1,128)}), f32[32,1,1152]{2,1,0:T(1,128)S(1)}, u32[]{:S(2)}, u32[]{:S(2)}) async-start(f32[32,1,1152]{2,1,0:T(1,128)} %bitcast.11), calls=%async_computation.2 | async-start | bytes 294912 | tf_op jit(solution)/shard_map/all_to_all | solution.py:320
  44.0 3.9 %collective-permute-start.2 = (f32[256,128]{1,0:T(8,128)S(1)}, f32[256,128]{1,0:T(8,128)S(1)}, u32[]{:S(2)}, u32[]{:S(2)}) collective-permute-start(f32[256,128]{1,0:T(8,128)S(1)} %bitcast.18), channel_id=1, source_target_pairs={{2,4},{4,2},{6,8},{8,6},{10,12},{12,10},{3,5},{5,3},{7,9},{9,7},{1... | collective-permute-start | bytes 393224 | tf_op jit(solution)/shard_map/ppermute | solution.py:305
  47.9 2.6 %collective-permute-start.3 = (f32[256,128]{1,0:T(8,128)S(1)}, f32[256,128]{1,0:T(8,128)S(1)}, u32[]{:S(2)}, u32[]{:S(2)}) collective-permute-start(f32[256,128]{1,0:T(8,128)S(1)} %bitcast.19), channel_id=1, source_target_pairs={{0,2},{2,0},{4,6},{6,4},{8,10},{10,8},{12,14},{14,12},{1,3},{3,1},... | collective-permute-start | bytes 393224 | tf_op jit(solution)/shard_map/ppermute | solution.py:313
  50.5 5.4 %collective-permute-start.4 = (f32[128,128]{1,0:T(8,128)S(1)}, f32[128,128]{1,0:T(8,128)S(1)}, u32[]{:S(2)}, u32[]{:S(2)}) collective-permute-start(f32[128,128]{1,0:T(8,128)S(1)} %get-tuple-element.38), channel_id=1, source_target_pairs={{0,1},{1,0},{2,3},{3,2},{4,5},{5,4},{6,7},{7,6},{8,9},{9,8},{10,11... | collective-permute-start | bytes 196616 | tf_op jit(solution)/shard_map/ppermute | solution.py:324
  55.9 0.0 collective-permute-done.2.outer
  56.0 0.9 %shard_map.85 = (f32[512,128]{1,0:T(8,128)S(1)}, f32[512,128]{1,0:T(8,128)S(1)}, f32[448,128]{1,0:T(8,128)S(1)}, f32[8,128]{1,0:T(8,128)S(1)}) custom-call(f32[256,128]{1,0:T(8,128)S(1)} %bitcast.20, f32[256,128]{1,0:T(8,128)S(1)} %collective-permute-done.2.outer, f32[80,128]{1,0:T(8,128)S(1)} %get-tuple-element.30.own.own2, f32[320,128]{1,0:T(8,128)S(1)} %bitcast.24, ...), custom_call_target="tpu_custom_call" | custom-call | tf_op jit(solution)/shard_map/pallas_call | solution.py:269
  56.8 0.0 collective-permute-done.3.inner
  56.8 2.4 %collective-permute-done.4.side = f32[128,128]{1,0:T(8,128)S(1)} collective-permute-done((f32[128,128]{1,0:T(8,128)S(1)}, f32[128,128]{1,0:T(8,128)S(1)}, u32[]{:S(2)}, u32[]{:S(2)}) %collective-permute-start.4) | collective-permute-done | bytes 65568 | tf_op jit(solution)/shard_map/ppermute | solution.py:324
  59.2 0.8 %shard_map.86 = (f32[512,128]{1,0:T(8,128)S(1)}, f32[512,128]{1,0:T(8,128)S(1)}) custom-call(f32[256,128]{1,0:T(8,128)S(1)} %bitcast.21, f32[256,128]{1,0:T(8,128)S(1)} %collective-permute-done.3.inner, f32[128,128]{1,0:T(8,128)S(1)} %collective-permute-done.4.side, f32[448,128]{1,0:T(8,128)S(1)} %get-tuple-element.39.tables, ...), custom_call_target="tpu_custom_call" | custom-call | tf_op jit(solution)/shard_map/pallas_call | solution.py:269
  60.0 0.0 all-to-all-done.2
  60.0 1.8 %shard_map.87 = f32[64,128]{1,0:T(8,128)} custom-call(f32[288,128]{1,0:T(8,128)S(1)} %bitcast.25, f32[64,128]{1,0:T(8,128)S(1)} %get-tuple-element.33.local, f32[512,128]{1,0:T(8,128)S(1)} %get-tuple-element.34.direct1, f32[512,128]{1,0:T(8,128)S(1)} %get-tuple-element.35.through1, f32[512,128]{1,0:T(8,128)S(1)} %get-tuple-element.40.direct2, ...), custom_call_target="tpu_custom_call" | custom-call | tf_op jit(solution)/shard_map/pallas_call | solution.py:269
Async XLA Ops:
  1.5 11.3 %copy-start = (f32[1,2,128,128]{3,2,1,0:T(8,128)S(1)}, f32[1,2,128,128]{3,2,1,0:T(8,128)}, u32[]{:S(2)}) copy-start(f32[1,2,128,128]{3,2,1,0:T(8,128)} %param.11) | copy-start | bytes 393220
  1.5 11.3 %copy-start.1 = (f32[32,1,2,128]{3,2,1,0:T(2,128)S(1)}, f32[32,1,2,128]{3,2,1,0:T(2,128)}, u32[]{:S(2)}) copy-start(f32[32,1,2,128]{3,2,1,0:T(2,128)} %param.9) | copy-start | bytes 98308
  1.5 11.3 %all-to-all-start = ((f32[4,64,128]{2,1,0:T(8,128)}), f32[4,64,128]{2,1,0:T(8,128)S(1)}, u32[]{:S(2)}, u32[]{:S(2)}) async-start(f32[4,64,128]{2,1,0:T(8,128)} %bitcast.29), calls=%async_computation | async-start | bytes 262144 | tf_op jit(solution)/shard_map/all_to_all | solution.py:298
  6.1 6.7 %collective-permute-start = (f32[64,128]{1,0:T(8,128)S(1)}, f32[64,128]{1,0:T(8,128)S(1)}, u32[]{:S(2)}, u32[]{:S(2)}) collective-permute-start(f32[64,128]{1,0:T(8,128)S(1)} %get-tuple-element.24.it), channel_id=1, source_target_pairs={{2,4},{4,2},{6,8},{8,6},{10,12},{12,10},{3,5},{5,3},{7,9},{9,7},{1... | collective-permute-start | bytes 98312 | tf_op jit(solution)/shard_map/ppermute | solution.py:302
  14.2 13.1 %all-to-all-start.1 = ((f32[4,80,128]{2,1,0:T(8,128)}), f32[4,80,128]{2,1,0:T(8,128)S(1)}, u32[]{:S(2)}, u32[]{:S(2)}) async-start(f32[4,80,128]{2,1,0:T(8,128)} %bitcast.9), calls=%async_computation.1 | async-start | bytes 327680 | tf_op jit(solution)/shard_map/all_to_all | solution.py:298
  19.0 8.3 %collective-permute-start.1 = (f32[80,128]{1,0:T(8,128)S(1)}, f32[80,128]{1,0:T(8,128)S(1)}, u32[]{:S(2)}, u32[]{:S(2)}) collective-permute-start(f32[80,128]{1,0:T(8,128)S(1)} %get-tuple-element.30.own.own2), channel_id=1, source_target_pairs={{2,4},{4,2},{6,8},{8,6},{10,12},{12,10},{3,5},{5,3},{7,9},{9,7},{1... | collective-permute-start | bytes 122888 | tf_op jit(solution)/shard_map/ppermute | solution.py:302
  28.3 31.8 %all-to-all-start.2 = ((f32[32,1,1152]{2,1,0:T(1,128)}), f32[32,1,1152]{2,1,0:T(1,128)S(1)}, u32[]{:S(2)}, u32[]{:S(2)}) async-start(f32[32,1,1152]{2,1,0:T(1,128)} %bitcast.11), calls=%async_computation.2 | async-start | bytes 294912 | tf_op jit(solution)/shard_map/all_to_all | solution.py:320
  44.0 11.9 %collective-permute-start.2 = (f32[256,128]{1,0:T(8,128)S(1)}, f32[256,128]{1,0:T(8,128)S(1)}, u32[]{:S(2)}, u32[]{:S(2)}) collective-permute-start(f32[256,128]{1,0:T(8,128)S(1)} %bitcast.18), channel_id=1, source_target_pairs={{2,4},{4,2},{6,8},{8,6},{10,12},{12,10},{3,5},{5,3},{7,9},{9,7},{1... | collective-permute-start | bytes 393224 | tf_op jit(solution)/shard_map/ppermute | solution.py:305
  47.9 8.9 %collective-permute-start.3 = (f32[256,128]{1,0:T(8,128)S(1)}, f32[256,128]{1,0:T(8,128)S(1)}, u32[]{:S(2)}, u32[]{:S(2)}) collective-permute-start(f32[256,128]{1,0:T(8,128)S(1)} %bitcast.19), channel_id=1, source_target_pairs={{0,2},{2,0},{4,6},{6,4},{8,10},{10,8},{12,14},{14,12},{1,3},{3,1},... | collective-permute-start | bytes 393224 | tf_op jit(solution)/shard_map/ppermute | solution.py:313
  50.5 8.7 %collective-permute-start.4 = (f32[128,128]{1,0:T(8,128)S(1)}, f32[128,128]{1,0:T(8,128)S(1)}, u32[]{:S(2)}, u32[]{:S(2)}) collective-permute-start(f32[128,128]{1,0:T(8,128)S(1)} %get-tuple-element.38), channel_id=1, source_target_pairs={{0,1},{1,0},{2,3},{3,2},{4,5},{5,4},{6,7},{7,6},{8,9},{9,8},{10,11... | collective-permute-start | bytes 196616 | tf_op jit(solution)/shard_map/ppermute | solution.py:324

commit v5 on v4

--- a/solution.py
+++ b/solution.py
@@ -7,7 +7,6 @@
 
 
 ALPHA = 0.05
-HIGHEST = lax.Precision.HIGHEST
 STEPS = 32
 BLOCKS = 32
 TILE = 128
@@ -19,16 +18,27 @@
 f32 = jnp.float32
 
 
+def halves(x):
+    high = x.astype(jnp.bfloat16)
+    return high, (x - high.astype(f32)).astype(jnp.bfloat16)
+
+
+def product(x, y, left, right):
+    (xh, xl), (yh, yl) = halves(x), halves(y)
+    one = lambda p, q: lax.dot_general(p, q, (((left,), (right,)), ((), ())), preferred_element_type=f32)
+    return one(xh, yh) + (one(xl, yh) + one(xh, yl))
+
+
 def mm(x, y):
-    return jnp.dot(x, y, precision=HIGHEST, preferred_element_type=f32)
+    return product(x, y, 1, 0)
 
 
 def mm_nt(x, y):
-    return lax.dot_general(x, y, (((1,), (1,)), ((), ())), precision=HIGHEST, preferred_element_type=f32)
+    return product(x, y, 1, 1)
 
 
 def mm_tn(x, y):
-    return lax.dot_general(x, y, (((0,), (0,)), ((), ())), precision=HIGHEST, preferred_element_type=f32)
+    return product(x, y, 0, 0)
 
 
 def rows_of(shape):
@@ -251,12 +261,12 @@
         decay, gain = params(coef, p)
         span = slice(2 * p * TILE, 2 * (p + 1) * TILE)
         beside = lambda x, j, k: jnp.concatenate([x[j], x[k]], axis=1)
-        product = lambda x, first, second: mm(beside(x, 2 + p, 1 - p), first[span, :]) + mm(
+        joined = lambda x, first, second: mm(beside(x, 2 + p, 1 - p), first[span, :]) + mm(
             beside(x, 4 + p, 6), second[span, :]
         )
-        ends = vector(7 + p) + factor * product(states, through1, through2)
+        ends = vector(7 + p) + factor * joined(states, through1, through2)
         entering = row_at(incoming(ends, decays[p : p + 1, :], table(7 + p)), block)
-        force = product(paths, direct1, direct2)
+        force = joined(paths, direct1, direct2)
         state = local[p * STEPS : (p + 1) * STEPS, :] + recurrence(force * gain, decay)
         state = state + table(p) * entering
         out[pl.ds(p, STEPS, stride=2), :] = mm_nt(state, basis)

time: 62.4 us -> 61.6 us (0.987)
  the two profiles are of different devices: /device:TPU:4 before, /device:TPU:2 now
where the time goes in v5:
time: 61.6 us; the launch traced here: 61 us
  starting transfers between devices  48.4 us (79%)
  Pallas kernels  6.38 us (10%)
  waiting for transfers between devices  6.13 us (10%)
    all_to_all x1, starting transfers between devices, on_device(): lax.all_to_all(flat, 'tm', split_axis=0, concat_axis=0, tiled=True, axis_...  14.2 us
    ppermute x2, starting transfers between devices, exchange(): return (quad.reshape(copies.shape), lax.ppermute(own, 'rows', swaps(1)))  13.4 us
    all_to_all x2, starting transfers between devices, exchange(): lax.all_to_all(copies.reshape(4, *own.shape), ('rows', 'cols'), split_axi...  8.54 us
    ppermute x1, starting transfers between devices, on_device(): side_basis = lax.ppermute(near_basis, 'cols', [(0, 1), (1, 0)])  5.44 us
    pallas_call x5, Pallas kernels, call(): pl.pallas_call(kernel, out_shape=shapes[0] if single else shapes, in_spec...  4.92 us
    ppermute x2, waiting for transfers between devices, exchange(): return (quad.reshape(copies.shape), lax.ppermute(own, 'rows', swaps(1)))  3.84 us
    ppermute x1, starting transfers between devices, on_device(): outer_basis = lax.ppermute(bas, 'rows', swaps(1))  3.61 us
    ppermute x1, starting transfers between devices, on_device(): inner_basis = lax.ppermute(rows_basis, 'rows', swaps(0))  3.16 us
  transfers between devices with their start and end apart: 8, of which 3 were waited for; matrix products, arithmetic and copies ran while one was open for 0% of the time, Pallas kernels for 2%

profile of v5, /device:TPU:2, one launch (start us, length us, event | category | flops | bytes accessed | tf_op | source)
XLA Modules:
  0.0 61.0 jit_solution(12219011394554825654)
XLA Ops:
  0.0 1.5 %shard_map.82 = (f32[256,128]{1,0:T(8,128)}, f32[64,128]{1,0:T(8,128)S(1)}, s32[8,128]{1,0:T(8,128)S(1)}, f32[8,128]{1,0:T(8,128)S(1)}, f32[2,128]{1,0:T(2,128)S(1)}, /*index=5*/f32[4,128]{1,0:T(4,128)S(1)}) custom-call(f32[64,128]{1,0:T(8,128)} %bitcast.30, s32[8,128]{1,0:T(8,128)} %bitcast.31, f32[8,128]{1,0:T(8,128)} %bitcast.32, f32[2,128]{1,0:T(2,128)} %bitcast.33, ...), custom_call_target="tpu_custom_call" | custom-call | tf_op jit(solution)/shard_map/pallas_call | solution.py:114
  1.5 0.0 copy-start
  1.5 0.0 copy-start.1
  1.5 4.6 %all-to-all-start = ((f32[4,64,128]{2,1,0:T(8,128)}), f32[4,64,128]{2,1,0:T(8,128)S(1)}, u32[]{:S(2)}, u32[]{:S(2)}) async-start(f32[4,64,128]{2,1,0:T(8,128)} %bitcast.29), calls=%async_computation | async-start | bytes 262144 | tf_op jit(solution)/shard_map/all_to_all | solution.py:308
  6.1 8.1 %collective-permute-start = (f32[64,128]{1,0:T(8,128)S(1)}, f32[64,128]{1,0:T(8,128)S(1)}, u32[]{:S(2)}, u32[]{:S(2)}) collective-permute-start(f32[64,128]{1,0:T(8,128)S(1)} %get-tuple-element.24.it), channel_id=1, source_target_pairs={{2,4},{4,2},{6,8},{8,6},{10,12},{12,10},{3,5},{5,3},{7,9},{9,7},{1... | collective-permute-start | bytes 98312 | tf_op jit(solution)/shard_map/ppermute | solution.py:312
  14.1 1.9 %collective-permute-done.outer = f32[64,128]{1,0:T(8,128)S(1)} collective-permute-done((f32[64,128]{1,0:T(8,128)S(1)}, f32[64,128]{1,0:T(8,128)S(1)}, u32[]{:S(2)}, u32[]{:S(2)}) %collective-permute-start) | collective-permute-done | bytes 32800 | tf_op jit(solution)/shard_map/ppermute | solution.py:312
  16.0 0.0 all-to-all-done
  16.0 0.0 copy-done
  16.0 0.0 copy-done.1
  16.0 1.2 %shard_map.83 = (f32[80,128]{1,0:T(8,128)S(1)}, f32[320,128]{1,0:T(8,128)}, f32[128,128]{1,0:T(8,128)S(1)}) custom-call(f32[64,128]{1,0:T(8,128)S(1)} %get-tuple-element.24.it, f32[64,128]{1,0:T(8,128)S(1)} %bitcast.27, f32[256,128]{1,0:T(8,128)S(1)} %bitcast.26, f32[64,128]{1,0:T(8,128)S(1)} %collective-permute-done.outer, f32[256,128]{1,0:T(8,128)S(1)} %bitcast.16, ...), custom_call_target="tpu_custom_call" | custom-call | tf_op jit(solution)/shard_map/pallas_call | solution.py:279
  17.2 3.9 %all-to-all-start.1 = ((f32[4,80,128]{2,1,0:T(8,128)}), f32[4,80,128]{2,1,0:T(8,128)S(1)}, u32[]{:S(2)}, u32[]{:S(2)}) async-start(f32[4,80,128]{2,1,0:T(8,128)} %bitcast.9), calls=%async_computation.1 | async-start | bytes 327680 | tf_op jit(solution)/shard_map/all_to_all | solution.py:308
  21.1 5.4 %collective-permute-start.1 = (f32[80,128]{1,0:T(8,128)S(1)}, f32[80,128]{1,0:T(8,128)S(1)}, u32[]{:S(2)}, u32[]{:S(2)}) collective-permute-start(f32[80,128]{1,0:T(8,128)S(1)} %get-tuple-element.30.own.own2), channel_id=1, source_target_pairs={{2,4},{4,2},{6,8},{8,6},{10,12},{12,10},{3,5},{5,3},{7,9},{9,7},{1... | collective-permute-start | bytes 122888 | tf_op jit(solution)/shard_map/ppermute | solution.py:312
  26.5 2.0 %collective-permute-done.1.outer.outer2 = f32[80,128]{1,0:T(8,128)S(1)} collective-permute-done((f32[80,128]{1,0:T(8,128)S(1)}, f32[80,128]{1,0:T(8,128)S(1)}, u32[]{:S(2)}, u32[]{:S(2)}) %collective-permute-start.1) | collective-permute-done | bytes 40992 | tf_op jit(solution)/shard_map/ppermute | solution.py:312
  28.5 0.0 all-to-all-done.1
  28.5 1.0 %shard_map.84 = (f32[64,128]{1,0:T(8,128)S(1)}, f32[288,128]{1,0:T(8,128)}) custom-call(f32[64,128]{1,0:T(8,128)S(1)} %bitcast.28, f32[80,128]{1,0:T(8,128)S(1)} %get-tuple-element.30.own.own2, f32[320,128]{1,0:T(8,128)S(1)} %bitcast.23, f32[80,128]{1,0:T(8,128)S(1)} %collective-permute-done.1.outer.outer2, f32[256,128]{1,0:T(8,128)S(1)} %bitcast.17, ...), custom_call_target="tpu_custom_call" | custom-call | tf_op jit(solution)/shard_map/pallas_call | solution.py:279
  29.5 14.2 %all-to-all-start.2 = ((f32[32,1,1152]{2,1,0:T(1,128)}), f32[32,1,1152]{2,1,0:T(1,128)S(1)}, u32[]{:S(2)}, u32[]{:S(2)}) async-start(f32[32,1,1152]{2,1,0:T(1,128)} %bitcast.11), calls=%async_computation.2 | async-start | bytes 294912 | tf_op jit(solution)/shard_map/all_to_all | solution.py:330
  43.7 3.6 %collective-permute-start.2 = (f32[256,128]{1,0:T(8,128)S(1)}, f32[256,128]{1,0:T(8,128)S(1)}, u32[]{:S(2)}, u32[]{:S(2)}) collective-permute-start(f32[256,128]{1,0:T(8,128)S(1)} %bitcast.18), channel_id=1, source_target_pairs={{2,4},{4,2},{6,8},{8,6},{10,12},{12,10},{3,5},{5,3},{7,9},{9,7},{1... | collective-permute-start | bytes 393224 | tf_op jit(solution)/shard_map/ppermute | solution.py:315
  47.3 3.2 %collective-permute-start.3 = (f32[256,128]{1,0:T(8,128)S(1)}, f32[256,128]{1,0:T(8,128)S(1)}, u32[]{:S(2)}, u32[]{:S(2)}) collective-permute-start(f32[256,128]{1,0:T(8,128)S(1)} %bitcast.19), channel_id=1, source_target_pairs={{0,2},{2,0},{4,6},{6,4},{8,10},{10,8},{12,14},{14,12},{1,3},{3,1},... | collective-permute-start | bytes 393224 | tf_op jit(solution)/shard_map/ppermute | solution.py:323
  50.5 5.4 %collective-permute-start.4 = (f32[128,128]{1,0:T(8,128)S(1)}, f32[128,128]{1,0:T(8,128)S(1)}, u32[]{:S(2)}, u32[]{:S(2)}) collective-permute-start(f32[128,128]{1,0:T(8,128)S(1)} %get-tuple-element.38), channel_id=1, source_target_pairs={{0,1},{1,0},{2,3},{3,2},{4,5},{5,4},{6,7},{7,6},{8,9},{9,8},{10,11... | collective-permute-start | bytes 196616 | tf_op jit(solution)/shard_map/ppermute | solution.py:334
  56.0 0.0 collective-permute-done.2.outer
  56.0 0.7 %shard_map.85 = (f32[512,128]{1,0:T(8,128)S(1)}, f32[512,128]{1,0:T(8,128)S(1)}, f32[448,128]{1,0:T(8,128)S(1)}, f32[8,128]{1,0:T(8,128)S(1)}) custom-call(f32[256,128]{1,0:T(8,128)S(1)} %bitcast.20, f32[256,128]{1,0:T(8,128)S(1)} %collective-permute-done.2.outer, f32[80,128]{1,0:T(8,128)S(1)} %get-tuple-element.30.own.own2, f32[320,128]{1,0:T(8,128)S(1)} %bitcast.24, ...), custom_call_target="tpu_custom_call" | custom-call | tf_op jit(solution)/shard_map/pallas_call | solution.py:279
  56.6 0.0 collective-permute-done.3.inner
  56.7 2.3 %collective-permute-done.4.side = f32[128,128]{1,0:T(8,128)S(1)} collective-permute-done((f32[128,128]{1,0:T(8,128)S(1)}, f32[128,128]{1,0:T(8,128)S(1)}, u32[]{:S(2)}, u32[]{:S(2)}) %collective-permute-start.4) | collective-permute-done | bytes 65568 | tf_op jit(solution)/shard_map/ppermute | solution.py:334
  58.9 0.7 %shard_map.86 = (f32[512,128]{1,0:T(8,128)S(1)}, f32[512,128]{1,0:T(8,128)S(1)}) custom-call(f32[256,128]{1,0:T(8,128)S(1)} %bitcast.21, f32[256,128]{1,0:T(8,128)S(1)} %collective-permute-done.3.inner, f32[128,128]{1,0:T(8,128)S(1)} %collective-permute-done.4.side, f32[448,128]{1,0:T(8,128)S(1)} %get-tuple-element.39.tables, ...), custom_call_target="tpu_custom_call" | custom-call | tf_op jit(solution)/shard_map/pallas_call | solution.py:279
  59.6 0.0 all-to-all-done.2
  59.6 1.4 %shard_map.87 = f32[64,128]{1,0:T(8,128)} custom-call(f32[288,128]{1,0:T(8,128)S(1)} %bitcast.25, f32[64,128]{1,0:T(8,128)S(1)} %get-tuple-element.33.local, f32[512,128]{1,0:T(8,128)S(1)} %get-tuple-element.34.direct1, f32[512,128]{1,0:T(8,128)S(1)} %get-tuple-element.35.through1, f32[512,128]{1,0:T(8,128)S(1)} %get-tuple-element.40.direct2, ...), custom_call_target="tpu_custom_call" | custom-call | tf_op jit(solution)/shard_map/pallas_call | solution.py:279
Async XLA Ops:
  1.5 14.6 %copy-start = (f32[1,2,128,128]{3,2,1,0:T(8,128)S(1)}, f32[1,2,128,128]{3,2,1,0:T(8,128)}, u32[]{:S(2)}) copy-start(f32[1,2,128,128]{3,2,1,0:T(8,128)} %param.11) | copy-start | bytes 393220
  1.5 14.6 %copy-start.1 = (f32[32,1,2,128]{3,2,1,0:T(2,128)S(1)}, f32[32,1,2,128]{3,2,1,0:T(2,128)}, u32[]{:S(2)}) copy-start(f32[32,1,2,128]{3,2,1,0:T(2,128)} %param.9) | copy-start | bytes 98308
  1.5 14.6 %all-to-all-start = ((f32[4,64,128]{2,1,0:T(8,128)}), f32[4,64,128]{2,1,0:T(8,128)S(1)}, u32[]{:S(2)}, u32[]{:S(2)}) async-start(f32[4,64,128]{2,1,0:T(8,128)} %bitcast.29), calls=%async_computation | async-start | bytes 262144 | tf_op jit(solution)/shard_map/all_to_all | solution.py:308
  6.1 10.0 %collective-permute-start = (f32[64,128]{1,0:T(8,128)S(1)}, f32[64,128]{1,0:T(8,128)S(1)}, u32[]{:S(2)}, u32[]{:S(2)}) collective-permute-start(f32[64,128]{1,0:T(8,128)S(1)} %get-tuple-element.24.it), channel_id=1, source_target_pairs={{2,4},{4,2},{6,8},{8,6},{10,12},{12,10},{3,5},{5,3},{7,9},{9,7},{1... | collective-permute-start | bytes 98312 | tf_op jit(solution)/shard_map/ppermute | solution.py:312
  17.2 11.3 %all-to-all-start.1 = ((f32[4,80,128]{2,1,0:T(8,128)}), f32[4,80,128]{2,1,0:T(8,128)S(1)}, u32[]{:S(2)}, u32[]{:S(2)}) async-start(f32[4,80,128]{2,1,0:T(8,128)} %bitcast.9), calls=%async_computation.1 | async-start | bytes 327680 | tf_op jit(solution)/shard_map/all_to_all | solution.py:308
  21.1 7.3 %collective-permute-start.1 = (f32[80,128]{1,0:T(8,128)S(1)}, f32[80,128]{1,0:T(8,128)S(1)}, u32[]{:S(2)}, u32[]{:S(2)}) collective-permute-start(f32[80,128]{1,0:T(8,128)S(1)} %get-tuple-element.30.own.own2), channel_id=1, source_target_pairs={{2,4},{4,2},{6,8},{8,6},{10,12},{12,10},{3,5},{5,3},{7,9},{9,7},{1... | collective-permute-start | bytes 122888 | tf_op jit(solution)/shard_map/ppermute | solution.py:312
  29.5 30.1 %all-to-all-start.2 = ((f32[32,1,1152]{2,1,0:T(1,128)}), f32[32,1,1152]{2,1,0:T(1,128)S(1)}, u32[]{:S(2)}, u32[]{:S(2)}) async-start(f32[32,1,1152]{2,1,0:T(1,128)} %bitcast.11), calls=%async_computation.2 | async-start | bytes 294912 | tf_op jit(solution)/shard_map/all_to_all | solution.py:330
  43.7 12.2 %collective-permute-start.2 = (f32[256,128]{1,0:T(8,128)S(1)}, f32[256,128]{1,0:T(8,128)S(1)}, u32[]{:S(2)}, u32[]{:S(2)}) collective-permute-start(f32[256,128]{1,0:T(8,128)S(1)} %bitcast.18), channel_id=1, source_target_pairs={{2,4},{4,2},{6,8},{8,6},{10,12},{12,10},{3,5},{5,3},{7,9},{9,7},{1... | collective-permute-start | bytes 393224 | tf_op jit(solution)/shard_map/ppermute | solution.py:315
  47.3 9.3 %collective-permute-start.3 = (f32[256,128]{1,0:T(8,128)S(1)}, f32[256,128]{1,0:T(8,128)S(1)}, u32[]{:S(2)}, u32[]{:S(2)}) collective-permute-start(f32[256,128]{1,0:T(8,128)S(1)} %bitcast.19), channel_id=1, source_target_pairs={{0,2},{2,0},{4,6},{6,4},{8,10},{10,8},{12,14},{14,12},{1,3},{3,1},... | collective-permute-start | bytes 393224 | tf_op jit(solution)/shard_map/ppermute | solution.py:323
  50.5 8.4 %collective-permute-start.4 = (f32[128,128]{1,0:T(8,128)S(1)}, f32[128,128]{1,0:T(8,128)S(1)}, u32[]{:S(2)}, u32[]{:S(2)}) collective-permute-start(f32[128,128]{1,0:T(8,128)S(1)} %get-tuple-element.38), channel_id=1, source_target_pairs={{0,1},{1,0},{2,3},{3,2},{4,5},{5,4},{6,7},{7,6},{8,9},{9,8},{10,11... | collective-permute-start | bytes 196616 | tf_op jit(solution)/shard_map/ppermute | solution.py:334

commit v6 on v5

--- a/solution.py
+++ b/solution.py
@@ -24,7 +24,7 @@
 
 
 def product(x, y, left, right):
-    (xh, xl), (yh, yl) = halves(x), halves(y)
+    (xh, xl), (yh, yl) = halves(x), y if isinstance(y, tuple) else halves(y)
     one = lambda p, q: lax.dot_general(p, q, (((left,), (right,)), ((), ())), preferred_element_type=f32)
     return one(xh, yh) + (one(xl, yh) + one(xh, yl))
 
@@ -198,7 +198,18 @@
     return pick(links), pick(cond)
 
 
-def kernel_m(bas, outer, own2, quad, outer2, links, cond, coef, direct, through, tables, decays):
+def store(ref, rows, high, low):
+    ref[rows, :] = high
+    at = ref.shape[0] // 2
+    ref[rows.start + at : rows.stop + at, :] = low
+
+
+def load(ref, rows):
+    at = ref.shape[0] // 2
+    return ref[rows, :], ref[rows.start + at : rows.stop + at, :]
+
+
+def kernel_m(bas, outer, own2, quad, outer2, links, cond, coef, direct, through, turned, tables, decays):
     odd = lax.axis_index("rows") % 2 == 1
     at = lambda x: x[1:2, :]
     both = lambda ref: [ref[p * PACK + STEPS : (p + 1) * PACK, :] for p in range(2)]
@@ -214,14 +225,17 @@
     decays[7:8, :] = jnp.zeros((1, TILE), f32)
     table = lambda k: tables[k * STEPS : (k + 1) * STEPS, :]
     for p in range(2):
+        store(turned, slice(p * TILE, (p + 1) * TILE), *halves(bas[p * TILE : (p + 1) * TILE, :].T))
         tile = lambda ref, q: ref[q * TILE : (q + 1) * TILE, :]
         near = 2 * (3 - p) + p
         for j, (neighbour, k, ties) in enumerate((
             (tile(outer, p), 2 + p, ties_of(links, cond, p, 2 + p, odd)),
             (tile(bas, 1 - p), 1 - p, ties_of(links, cond, near, near, odd)),
         )):
+            made = matrices(p, neighbour, table(k), ties, None, bas, coef)
             rows = slice((2 * p + j) * TILE, (2 * p + j + 1) * TILE)
-            direct[rows, :], through[rows, :] = matrices(p, neighbour, table(k), ties, None, bas, coef)
+            store(direct, rows, *halves(made[0]))
+            store(through, rows, *halves(made[1]))
 
 
 def kernel_n(bas, inner, side, tables, links, cond, coef, direct, through):
@@ -235,8 +249,10 @@
             (inner[p * TILE : (p + 1) * TILE, :], 4 + p, ties_of(links, cond, 2 + p, p, odd), None),
             (side[...], 6, ties_of(links, cond, far, far, odd), outside),
         )):
+            made = matrices(p, neighbour, table(k), ties, mask, bas, coef)
             rows = slice((2 * p + j) * TILE, (2 * p + j + 1) * TILE)
-            direct[rows, :], through[rows, :] = matrices(p, neighbour, table(k), ties, mask, bas, coef)
+            store(direct, rows, *halves(made[0]))
+            store(through, rows, *halves(made[1]))
 
 
 def incoming(ends, block_decay, scaled_powers):
@@ -249,7 +265,7 @@
     return jnp.sum(jnp.where(rows_of(x.shape) == index, x, 0.0), axis=0, keepdims=True)
 
 
-def kernel_c(received, local, direct1, through1, direct2, through2, tables, decays, bas, coef, out):
+def kernel_c(received, local, direct1, through1, direct2, through2, turned, tables, decays, coef, out):
     block = lax.axis_index("tm")
     vector = lambda k: pltpu.roll(received[pl.ds(k, BLOCKS, stride=VECS), :], FIRST, 0)
     table = lambda k: tables[k * STEPS : (k + 1) * STEPS, :]
@@ -257,24 +273,23 @@
     paths = [table(k) * row_at(states[k], block) for k in range(7)]
     factor = jnp.where(rows_of((BLOCKS, TILE)) == BLOCKS - 1, ALPHA, 1.0)
     for p in range(2):
-        basis = bas[p * TILE : (p + 1) * TILE, :]
         decay, gain = params(coef, p)
         span = slice(2 * p * TILE, 2 * (p + 1) * TILE)
         beside = lambda x, j, k: jnp.concatenate([x[j], x[k]], axis=1)
-        joined = lambda x, first, second: mm(beside(x, 2 + p, 1 - p), first[span, :]) + mm(
-            beside(x, 4 + p, 6), second[span, :]
+        joined = lambda x, first, second: mm(beside(x, 2 + p, 1 - p), load(first, span)) + mm(
+            beside(x, 4 + p, 6), load(second, span)
         )
         ends = vector(7 + p) + factor * joined(states, through1, through2)
         entering = row_at(incoming(ends, decays[p : p + 1, :], table(7 + p)), block)
         force = joined(paths, direct1, direct2)
         state = local[p * STEPS : (p + 1) * STEPS, :] + recurrence(force * gain, decay)
         state = state + table(p) * entering
-        out[pl.ds(p, STEPS, stride=2), :] = mm_nt(state, basis)
+        out[pl.ds(p, STEPS, stride=2), :] = mm(state, load(turned, slice(p * TILE, (p + 1) * TILE)))
 
 
 def call(kernel, outs, *args, last=False):
     vmem = pl.BlockSpec(memory_space=pltpu.VMEM)
-    shapes = [jax.ShapeDtypeStruct(out, f32) if last else pltpu.VMEM(out, f32) for out in outs]
+    shapes = [jax.ShapeDtypeStruct(out[:2], f32) if last else pltpu.VMEM(out[:2], *(out[2:] or (f32,))) for out in outs]
     single = len(outs) == 1
     return pl.pallas_call(
         kernel,
@@ -332,16 +347,16 @@
     ).reshape(BLOCKS * VECS, TILE)
     near_basis, _ = lax.optimization_barrier((near_basis, send))
     side_basis = lax.ppermute(near_basis, "cols", [(0, 1), (1, 0)])
-    pair_shape, table_shape = (4 * TILE, TILE), (14 * STEPS, TILE)
-    direct1, through1, tables, decays = call(
+    pair_shape, table_shape = (8 * TILE, TILE, jnp.bfloat16), (14 * STEPS, TILE)
+    direct1, through1, turned, tables, decays = call(
         kernel_m,
-        [pair_shape, pair_shape, table_shape, (8, TILE)],
+        [pair_shape, pair_shape, (4 * TILE, TILE, jnp.bfloat16), table_shape, (8, TILE)],
         bas, outer_basis, own2, quad, outer2, links, cond, coef,
     )
     direct2, through2 = call(
         kernel_n, [pair_shape, pair_shape], bas, inner_basis, side_basis, tables, links, cond, coef
     )
-    out = call(kernel_c, [(2 * STEPS, TILE)], received, local, direct1, through1, direct2, through2, tables, decays, bas, coef, last=True)
+    out = call(kernel_c, [(2 * STEPS, TILE)], received, local, direct1, through1, direct2, through2, turned, tables, decays, coef, last=True)
     return out.reshape(iterate.shape)
 
 

time: 61.6 us -> 61.5 us (level)
  no operation moved by 1% of the time
where the time goes in v6:
time: 61.5 us; the launch traced here: 60.9 us
  starting transfers between devices  48.4 us (79%)
  Pallas kernels  6.29 us (10%)
  waiting for transfers between devices  6.12 us (10%)
    all_to_all x1, starting transfers between devices, on_device(): lax.all_to_all(flat, 'tm', split_axis=0, concat_axis=0, tiled=True, axis_...  14.2 us
    ppermute x2, starting transfers between devices, exchange(): return (quad.reshape(copies.shape), lax.ppermute(own, 'rows', swaps(1)))  13.4 us
    all_to_all x2, starting transfers between devices, exchange(): lax.all_to_all(copies.reshape(4, *own.shape), ('rows', 'cols'), split_axi...  8.54 us
    ppermute x1, starting transfers between devices, on_device(): side_basis = lax.ppermute(near_basis, 'cols', [(0, 1), (1, 0)])  5.44 us
    pallas_call x5, Pallas kernels, call(): pl.pallas_call(kernel, out_shape=shapes[0] if single else shapes, in_spec...  4.83 us
    ppermute x2, waiting for transfers between devices, exchange(): return (quad.reshape(copies.shape), lax.ppermute(own, 'rows', swaps(1)))  3.84 us
    ppermute x1, starting transfers between devices, on_device(): outer_basis = lax.ppermute(bas, 'rows', swaps(1))  3.61 us
    ppermute x1, starting transfers between devices, on_device(): inner_basis = lax.ppermute(rows_basis, 'rows', swaps(0))  3.16 us
  transfers between devices with their start and end apart: 8, of which 3 were waited for; matrix products, arithmetic and copies ran while one was open for 0% of the time, Pallas kernels for 2%

profile of v6, /device:TPU:2, one launch (start us, length us, event | category | flops | bytes accessed | tf_op | source)
XLA Modules:
  0.0 60.9 jit_solution(10525446729548850316)
XLA Ops:
  0.0 1.5 %shard_map.82 = (f32[256,128]{1,0:T(8,128)}, f32[64,128]{1,0:T(8,128)S(1)}, s32[8,128]{1,0:T(8,128)S(1)}, f32[8,128]{1,0:T(8,128)S(1)}, f32[2,128]{1,0:T(2,128)S(1)}, /*index=5*/f32[4,128]{1,0:T(4,128)S(1)}) custom-call(f32[64,128]{1,0:T(8,128)} %bitcast.29, s32[8,128]{1,0:T(8,128)} %bitcast.30, f32[8,128]{1,0:T(8,128)} %bitcast.31, f32[2,128]{1,0:T(2,128)} %bitcast.32, ...), custom_call_target="tpu_custom_call" | custom-call | tf_op jit(solution)/shard_map/pallas_call | solution.py:114
  1.5 0.0 copy-start
  1.5 0.0 copy-start.1
  1.5 4.6 %all-to-all-start = ((f32[4,64,128]{2,1,0:T(8,128)}), f32[4,64,128]{2,1,0:T(8,128)S(1)}, u32[]{:S(2)}, u32[]{:S(2)}) async-start(f32[4,64,128]{2,1,0:T(8,128)} %bitcast.28), calls=%async_computation | async-start | bytes 262144 | tf_op jit(solution)/shard_map/all_to_all | solution.py:323
  6.1 8.1 %collective-permute-start = (f32[64,128]{1,0:T(8,128)S(1)}, f32[64,128]{1,0:T(8,128)S(1)}, u32[]{:S(2)}, u32[]{:S(2)}) collective-permute-start(f32[64,128]{1,0:T(8,128)S(1)} %get-tuple-element.25.it), channel_id=1, source_target_pairs={{2,4},{4,2},{6,8},{8,6},{10,12},{12,10},{3,5},{5,3},{7,9},{9,7},{1... | collective-permute-start | bytes 98312 | tf_op jit(solution)/shard_map/ppermute | solution.py:327
  14.1 1.9 %collective-permute-done.outer = f32[64,128]{1,0:T(8,128)S(1)} collective-permute-done((f32[64,128]{1,0:T(8,128)S(1)}, f32[64,128]{1,0:T(8,128)S(1)}, u32[]{:S(2)}, u32[]{:S(2)}) %collective-permute-start) | collective-permute-done | bytes 32800 | tf_op jit(solution)/shard_map/ppermute | solution.py:327
  16.0 0.0 all-to-all-done
  16.0 0.0 copy-done
  16.0 0.0 copy-done.1
  16.0 1.2 %shard_map.83 = (f32[80,128]{1,0:T(8,128)S(1)}, f32[320,128]{1,0:T(8,128)}, f32[128,128]{1,0:T(8,128)S(1)}) custom-call(f32[64,128]{1,0:T(8,128)S(1)} %get-tuple-element.25.it, f32[64,128]{1,0:T(8,128)S(1)} %bitcast.26, f32[256,128]{1,0:T(8,128)S(1)} %bitcast.25, f32[64,128]{1,0:T(8,128)S(1)} %collective-permute-done.outer, f32[256,128]{1,0:T(8,128)S(1)} %bitcast.16, ...), custom_call_target="tpu_custom_call" | custom-call | tf_op jit(solution)/shard_map/pallas_call | solution.py:294
  17.2 3.9 %all-to-all-start.1 = ((f32[4,80,128]{2,1,0:T(8,128)}), f32[4,80,128]{2,1,0:T(8,128)S(1)}, u32[]{:S(2)}, u32[]{:S(2)}) async-start(f32[4,80,128]{2,1,0:T(8,128)} %bitcast.9), calls=%async_computation.1 | async-start | bytes 327680 | tf_op jit(solution)/shard_map/all_to_all | solution.py:323
  21.1 5.4 %collective-permute-start.1 = (f32[80,128]{1,0:T(8,128)S(1)}, f32[80,128]{1,0:T(8,128)S(1)}, u32[]{:S(2)}, u32[]{:S(2)}) collective-permute-start(f32[80,128]{1,0:T(8,128)S(1)} %get-tuple-element.31.own.own2), channel_id=1, source_target_pairs={{2,4},{4,2},{6,8},{8,6},{10,12},{12,10},{3,5},{5,3},{7,9},{9,7},{1... | collective-permute-start | bytes 122888 | tf_op jit(solution)/shard_map/ppermute | solution.py:327
  26.5 2.0 %collective-permute-done.1.outer.outer2 = f32[80,128]{1,0:T(8,128)S(1)} collective-permute-done((f32[80,128]{1,0:T(8,128)S(1)}, f32[80,128]{1,0:T(8,128)S(1)}, u32[]{:S(2)}, u32[]{:S(2)}) %collective-permute-start.1) | collective-permute-done | bytes 40992 | tf_op jit(solution)/shard_map/ppermute | solution.py:327
  28.5 0.0 all-to-all-done.1
  28.5 1.0 %shard_map.84 = (f32[64,128]{1,0:T(8,128)S(1)}, f32[288,128]{1,0:T(8,128)}) custom-call(f32[64,128]{1,0:T(8,128)S(1)} %bitcast.27, f32[80,128]{1,0:T(8,128)S(1)} %get-tuple-element.31.own.own2, f32[320,128]{1,0:T(8,128)S(1)} %bitcast.22, f32[80,128]{1,0:T(8,128)S(1)} %collective-permute-done.1.outer.outer2, f32[256,128]{1,0:T(8,128)S(1)} %bitcast.17, ...), custom_call_target="tpu_custom_call" | custom-call | tf_op jit(solution)/shard_map/pallas_call | solution.py:294
  29.5 14.2 %all-to-all-start.2 = ((f32[32,1,1152]{2,1,0:T(1,128)}), f32[32,1,1152]{2,1,0:T(1,128)S(1)}, u32[]{:S(2)}, u32[]{:S(2)}) async-start(f32[32,1,1152]{2,1,0:T(1,128)} %bitcast.11), calls=%async_computation.2 | async-start | bytes 294912 | tf_op jit(solution)/shard_map/all_to_all | solution.py:345
  43.7 3.6 %collective-permute-start.2 = (f32[256,128]{1,0:T(8,128)S(1)}, f32[256,128]{1,0:T(8,128)S(1)}, u32[]{:S(2)}, u32[]{:S(2)}) collective-permute-start(f32[256,128]{1,0:T(8,128)S(1)} %bitcast.18), channel_id=1, source_target_pairs={{2,4},{4,2},{6,8},{8,6},{10,12},{12,10},{3,5},{5,3},{7,9},{9,7},{1... | collective-permute-start | bytes 393224 | tf_op jit(solution)/shard_map/ppermute | solution.py:330
  47.3 3.2 %collective-permute-start.3 = (f32[256,128]{1,0:T(8,128)S(1)}, f32[256,128]{1,0:T(8,128)S(1)}, u32[]{:S(2)}, u32[]{:S(2)}) collective-permute-start(f32[256,128]{1,0:T(8,128)S(1)} %bitcast.19), channel_id=1, source_target_pairs={{0,2},{2,0},{4,6},{6,4},{8,10},{10,8},{12,14},{14,12},{1,3},{3,1},... | collective-permute-start | bytes 393224 | tf_op jit(solution)/shard_map/ppermute | solution.py:338
  50.5 5.4 %collective-permute-start.4 = (f32[128,128]{1,0:T(8,128)S(1)}, f32[128,128]{1,0:T(8,128)S(1)}, u32[]{:S(2)}, u32[]{:S(2)}) collective-permute-start(f32[128,128]{1,0:T(8,128)S(1)} %get-tuple-element.39), channel_id=1, source_target_pairs={{0,1},{1,0},{2,3},{3,2},{4,5},{5,4},{6,7},{7,6},{8,9},{9,8},{10,11... | collective-permute-start | bytes 196616 | tf_op jit(solution)/shard_map/ppermute | solution.py:349
  56.0 0.0 collective-permute-done.2.outer
  56.0 0.7 %shard_map.85 = (bf16[1024,128]{1,0:T(8,128)(2,1)S(1)}, bf16[1024,128]{1,0:T(8,128)(2,1)S(1)}, bf16[512,128]{1,0:T(8,128)(2,1)S(1)}, f32[448,128]{1,0:T(8,128)S(1)}, f32[8,128]{1,0:T(8,128)S(1)}) custom-call(f32[256,128]{1,0:T(8,128)S(1)} %bitcast.20, f32[256,128]{1,0:T(8,128)S(1)} %collective-permute-done.2.outer, ...), custom_call_target="tpu_custom_call" | custom-call | tf_op jit(solution)/shard_map/pallas_call | solution.py:294
  56.6 0.0 collective-permute-done.3.inner
  56.7 2.3 %collective-permute-done.4.side = f32[128,128]{1,0:T(8,128)S(1)} collective-permute-done((f32[128,128]{1,0:T(8,128)S(1)}, f32[128,128]{1,0:T(8,128)S(1)}, u32[]{:S(2)}, u32[]{:S(2)}) %collective-permute-start.4) | collective-permute-done | bytes 65568 | tf_op jit(solution)/shard_map/ppermute | solution.py:349
  58.9 0.7 %shard_map.86 = (bf16[1024,128]{1,0:T(8,128)(2,1)S(1)}, bf16[1024,128]{1,0:T(8,128)(2,1)S(1)}) custom-call(f32[256,128]{1,0:T(8,128)S(1)} %bitcast.21, f32[256,128]{1,0:T(8,128)S(1)} %collective-permute-done.3.inner, f32[128,128]{1,0:T(8,128)S(1)} %collective-permute-done.4.side, f32[448,128]{1,0:T(8,128)S(1)} %get-tuple-element.40.tables, ...), custom_call_target="tpu_custom_call" | custom-call | tf_op jit(solution)/shard_map/pallas_call | solution.py:294
  59.6 0.0 all-to-all-done.2
  59.6 1.3 %shard_map.87 = f32[64,128]{1,0:T(8,128)} custom-call(f32[288,128]{1,0:T(8,128)S(1)} %bitcast.24, f32[64,128]{1,0:T(8,128)S(1)} %get-tuple-element.34.local, bf16[1024,128]{1,0:T(8,128)(2,1)S(1)} %get-tuple-element.35.direct1, bf16[1024,128]{1,0:T(8,128)(2,1)S(1)} %get-tuple-element.36.through1, bf16[1024,128]{1,0:T(8,128)(2,1)S(1)} %get-tuple-element.41.direct2, ...), custom_call_target="tpu_custom_call" | custom-call | tf_op jit(solution)/shard_map/pallas_call | solution.py:294
Async XLA Ops:
  1.5 14.6 %copy-start = (f32[1,2,128,128]{3,2,1,0:T(8,128)S(1)}, f32[1,2,128,128]{3,2,1,0:T(8,128)}, u32[]{:S(2)}) copy-start(f32[1,2,128,128]{3,2,1,0:T(8,128)} %param.11) | copy-start | bytes 393220
  1.5 14.6 %copy-start.1 = (f32[32,1,2,128]{3,2,1,0:T(2,128)S(1)}, f32[32,1,2,128]{3,2,1,0:T(2,128)}, u32[]{:S(2)}) copy-start(f32[32,1,2,128]{3,2,1,0:T(2,128)} %param.9) | copy-start | bytes 98308
  1.5 14.6 %all-to-all-start = ((f32[4,64,128]{2,1,0:T(8,128)}), f32[4,64,128]{2,1,0:T(8,128)S(1)}, u32[]{:S(2)}, u32[]{:S(2)}) async-start(f32[4,64,128]{2,1,0:T(8,128)} %bitcast.28), calls=%async_computation | async-start | bytes 262144 | tf_op jit(solution)/shard_map/all_to_all | solution.py:323
  6.1 10.0 %collective-permute-start = (f32[64,128]{1,0:T(8,128)S(1)}, f32[64,128]{1,0:T(8,128)S(1)}, u32[]{:S(2)}, u32[]{:S(2)}) collective-permute-start(f32[64,128]{1,0:T(8,128)S(1)} %get-tuple-element.25.it), channel_id=1, source_target_pairs={{2,4},{4,2},{6,8},{8,6},{10,12},{12,10},{3,5},{5,3},{7,9},{9,7},{1... | collective-permute-start | bytes 98312 | tf_op jit(solution)/shard_map/ppermute | solution.py:327
  17.2 11.3 %all-to-all-start.1 = ((f32[4,80,128]{2,1,0:T(8,128)}), f32[4,80,128]{2,1,0:T(8,128)S(1)}, u32[]{:S(2)}, u32[]{:S(2)}) async-start(f32[4,80,128]{2,1,0:T(8,128)} %bitcast.9), calls=%async_computation.1 | async-start | bytes 327680 | tf_op jit(solution)/shard_map/all_to_all | solution.py:323
  21.1 7.3 %collective-permute-start.1 = (f32[80,128]{1,0:T(8,128)S(1)}, f32[80,128]{1,0:T(8,128)S(1)}, u32[]{:S(2)}, u32[]{:S(2)}) collective-permute-start(f32[80,128]{1,0:T(8,128)S(1)} %get-tuple-element.31.own.own2), channel_id=1, source_target_pairs={{2,4},{4,2},{6,8},{8,6},{10,12},{12,10},{3,5},{5,3},{7,9},{9,7},{1... | collective-permute-start | bytes 122888 | tf_op jit(solution)/shard_map/ppermute | solution.py:327
  29.5 30.1 %all-to-all-start.2 = ((f32[32,1,1152]{2,1,0:T(1,128)}), f32[32,1,1152]{2,1,0:T(1,128)S(1)}, u32[]{:S(2)}, u32[]{:S(2)}) async-start(f32[32,1,1152]{2,1,0:T(1,128)} %bitcast.11), calls=%async_computation.2 | async-start | bytes 294912 | tf_op jit(solution)/shard_map/all_to_all | solution.py:345
  43.7 12.2 %collective-permute-start.2 = (f32[256,128]{1,0:T(8,128)S(1)}, f32[256,128]{1,0:T(8,128)S(1)}, u32[]{:S(2)}, u32[]{:S(2)}) collective-permute-start(f32[256,128]{1,0:T(8,128)S(1)} %bitcast.18), channel_id=1, source_target_pairs={{2,4},{4,2},{6,8},{8,6},{10,12},{12,10},{3,5},{5,3},{7,9},{9,7},{1... | collective-permute-start | bytes 393224 | tf_op jit(solution)/shard_map/ppermute | solution.py:330
  47.3 9.3 %collective-permute-start.3 = (f32[256,128]{1,0:T(8,128)S(1)}, f32[256,128]{1,0:T(8,128)S(1)}, u32[]{:S(2)}, u32[]{:S(2)}) collective-permute-start(f32[256,128]{1,0:T(8,128)S(1)} %bitcast.19), channel_id=1, source_target_pairs={{0,2},{2,0},{4,6},{6,4},{8,10},{10,8},{12,14},{14,12},{1,3},{3,1},... | collective-permute-start | bytes 393224 | tf_op jit(solution)/shard_map/ppermute | solution.py:338
  50.5 8.4 %collective-permute-start.4 = (f32[128,128]{1,0:T(8,128)S(1)}, f32[128,128]{1,0:T(8,128)S(1)}, u32[]{:S(2)}, u32[]{:S(2)}) collective-permute-start(f32[128,128]{1,0:T(8,128)S(1)} %get-tuple-element.39), channel_id=1, source_target_pairs={{0,1},{1,0},{2,3},{3,2},{4,5},{5,4},{6,7},{7,6},{8,9},{9,8},{10,11... | collective-permute-start | bytes 196616 | tf_op jit(solution)/shard_map/ppermute | solution.py:349
